TPU v7x, 128 devices: a whole 4x4x4 slice. The times are simulated.
128 devices in a mesh: row: 16 (over x, y), col: 8 (over z, core).
Axes of the slice: x: 4, y: 4, z: 4, core: 2. Of those that a mesh axis runs over, the one named last changes fastest.
Arguments:
- states: bfloat16 [128, 2, 8, 5376], P(None, None, None, 'row'), may hold values from -6 to 6
- subject_pos: int32 [128, 2], replicated, may hold values from 0 to 7
- gate_weight: bfloat16 [5376, 8, 2688], P('row', 'col'), may hold values from -0.078125 to 0.078125
- up_weight: bfloat16 [5376, 8, 2688], P('row', 'col'), may hold values from -0.078125 to 0.078125
- down_weight: bfloat16 [16, 8, 168, 5376], P('row', 'col'), may hold values from -0.0390625 to 0.0390625
- covariance: float32 [21504, 8, 2688], P('row', 'col'), as said below
- targets: float32 [5376, 128], P(('row', 'col')), may hold values from -24 to 24
Outputs:
- update: bfloat16 [16, 8, 168, 5376], P('row', 'col')
Inputs may be any that keep to these rules, and one draw needn't show every extreme that they name: `covariance`: read as an 21504 x 21504 matrix (entry (i, b, a * 168 + j) in column a * 8 * 168 + b * 168 + j), it is symmetric and positive definite.
All inputs are finite; a program needn't handle non-finite values.
Results may differ from a plain program's by a relative error of at most 0.0016.
Values sent between devices are 32-bit elements; how exact they have to be, the bound alone decides.
A program may use at most 128 MiB of HBM per device.

v0:
```python
import math

import jax
import jax.numpy as jnp
from jax import lax
from jax.sharding import PartitionSpec as P

FF = 21504
ITERS = 2


def split_up(array, dim, peers):
    dims = array.shape
    tiles = array.reshape(*dims[:dim], peers, dims[dim] // peers, *dims[dim + 1 :])
    return jnp.moveaxis(tiles, dim, 0)


def own_tiles(array, axis, dim):
    peers = lax.axis_size(axis)
    tiles = split_up(array, dim, peers)
    lines = tiles.reshape(peers, -1)
    span = max(16, -(-lines.shape[1] // 1024) * 8)
    lines = jnp.pad(lines, ((0, 0), (0, span * 128 - lines.shape[1]))).reshape(-1, 128)
    own = lax.psum_scatter(lines, axis, scatter_dimension=0, tiled=True)
    return own.reshape(-1)[: tiles[0].size].reshape(tiles.shape[1:])


def copy_for_each(array, axis):
    peers = lax.axis_size(axis)
    return lax.all_to_all(
        jnp.broadcast_to(array[None], (peers, *array.shape)), axis, 0, 0, tiled=True
    )


def joined_along(tiles, dim):
    dims = list(tiles.shape[1:])
    dims[dim] *= tiles.shape[0]
    return jnp.moveaxis(tiles, 0, dim).reshape(dims)


def gathered_copies(array, axis, dim):
    tiles = copy_for_each(array, axis)
    return joined_along(tiles, dim)


def gathered_total(array, axis):
    tiles = lax.all_gather(array, axis)
    return tiles.sum(axis=0)


def over_copies(array, axis):
    return copy_for_each(array, axis).sum(axis=0)


def inner(left, right):
    return lax.dot_general(
        left,
        right,
        (((0,), (0,)), ((), ())),
        precision=lax.Precision.HIGHEST,
        preferred_element_type=jnp.float32,
    )


def times_small(left, small):
    return jnp.dot(left, small, precision=lax.Precision.HIGHEST, preferred_element_type=jnp.float32)


def small_solve(matrix, right):
    factor = jnp.linalg.cholesky(matrix)
    return jax.scipy.linalg.cho_solve((factor, True), right)


def symmetric(matrix):
    return 0.5 * (matrix + matrix.T)


def body(states, subject_pos, gate_weight, up_weight, down_weight, covariance, targets):
    seq_len = states.shape[2]
    marks = lax.broadcasted_iota(jnp.int32, (1, 1, seq_len, 1), 2) == subject_pos[:, :, None, None]
    chosen = jnp.sum(jnp.where(marks, states, jnp.zeros_like(states)), axis=2)
    token_rows = chosen.reshape(-1, chosen.shape[-1])
    count_tokens = token_rows.shape[0]
    gate_flat = gate_weight.reshape(gate_weight.shape[0], -1)
    up_flat = up_weight.reshape(up_weight.shape[0], -1)
    contract = (((0,), (1,)), ((), ()))
    piece_rows = down_weight.shape[2]
    edit_count = subject_pos.shape[0]
    gate_part = lax.dot_general(gate_flat, token_rows, contract, preferred_element_type=jnp.float32)
    up_part = lax.dot_general(up_flat, token_rows, contract, preferred_element_type=jnp.float32)
    summed = lax.psum_scatter(
        jnp.concatenate([gate_part, up_part], axis=1), "row", scatter_dimension=0, tiled=True
    )
    hidden = jax.nn.silu(summed[:, :count_tokens]) * summed[:, count_tokens:]
    keys = jnp.mean(hidden.reshape(piece_rows, edit_count, -1), axis=2)
    keys_half = keys.astype(jnp.bfloat16)
    down_flat = down_weight.reshape(piece_rows, -1)
    current = own_tiles(
        lax.dot_general(
            down_flat, keys_half, (((0,), (0,)), ((), ())), preferred_element_type=jnp.float32
        ),
        ("row", "col"),
        0,
    )
    residual_t = targets - current
    basis = 4.0 / math.sqrt(FF) * keys
    cov_flat = covariance.reshape(covariance.shape[0], -1)
    column = lax.axis_index("col")
    basis = gathered_copies(basis, "col", 0)

    def own_piece(field):
        return lax.dynamic_slice_in_dim(field, column * piece_rows, piece_rows, 0)

    def summed_small(terms):
        return over_copies(terms, "row")

    solution = jnp.zeros_like(basis)
    resid = basis
    direction = basis
    norm_now = symmetric(summed_small(inner(resid, resid)))
    for step in range(ITERS):
        projected = summed_small(inner(basis, direction))
        partial_value = jnp.dot(
            cov_flat,
            gathered_copies(own_piece(direction), "row", 0),
            precision=lax.Precision.HIGHEST,
            preferred_element_type=jnp.float32,
        )
        image = gathered_total(partial_value, "col") + times_small(basis, projected)
        curvature = symmetric(summed_small(inner(direction, image)))
        alpha = small_solve(curvature, norm_now)
        solution = solution + times_small(direction, alpha)
        resid = resid - times_small(image, alpha)
        if step + 1 < ITERS:
            norm_next = symmetric(summed_small(inner(resid, resid)))
            beta = small_solve(norm_now, norm_next)
            direction = resid + times_small(direction, beta)
            norm_now = norm_next
    own_solution = own_piece(solution)
    update = lax.dot_general(
        own_solution,
        lax.all_gather(residual_t, ("row", "col"), axis=0, tiled=True),
        (((1,), (1,)), ((), ())),
        precision=lax.Precision.HIGHEST,
        preferred_element_type=jnp.float32,
    )
    return update.astype(jnp.bfloat16).reshape(1, 1, piece_rows, -1)


def solution(mesh):
    return jax.shard_map(
        body,
        mesh=mesh,
        in_specs=(
            P(None, None, None, "row"),
            P(),
            P("row", "col", None),
            P("row", "col", None),
            P("row", "col", None, None),
            P("row", "col", None),
            P(("row", "col"), None),
        ),
        out_specs=P("row", "col", None, None),
        check_vma=False,
    )
```

profile of v0, /device:TPU:1, one launch (start us, length us, event | category | flops | bytes accessed | tf_op | source)
XLA Modules:
  0.0 622.9 jit_solution(3397620750936051683)
XLA Ops:
  6.5 0.8 iota_compare_fusion.2
  7.4 1.6 select_reduce_fusion
  9.4 0.9 convolution_bitcast_fusion.1
  10.8 0.9 convolution_bitcast_fusion.2
  11.7 2.8 pad_maximum_fusion
  16.4 116.4 %all-reduce.4.cloned.1.call-done = f32[2688,512]{0,1:T(8,128)} async-done(((f32[2688,512]{0,1:T(8,128)}), f32[2688,512]{0,1:T(8,128)}) %all-reduce.4.cloned.1.call-update) | async-done | bytes 5505040
  132.9 1.3 dynamic-slice_multiply_fusion
  134.8 0.9 broadcast_in_dim.28
  135.7 5.1 all-to-all-start
  140.8 11.2 %all-to-all-done = f32[8,168,128]{2,1,0:T(8,128)S(1)} async-done(((f32[8,168,128]{2,1,0:T(8,128)}), f32[8,168,128]{2,1,0:T(8,128)S(1)}, u32[]{:S(2)}, u32[]{:S(2)}) %all-to-all-start) | async-done | bytes 688160 | tf_op jit(solution)/shard_map/all_to_all | solution.py:30
  152.1 24.1 %all_to_all.41 = f32[16,168,128]{2,1,0:T(8,128)S(1)} all-to-all(f32[16,168,128]{2,1,0:T(8,128)S(1)} %broadcast_in_dim.30), channel_id=1, replica_groups=mesh['row'=16,'col'=8] {'row'}, dimensions={0} | all-to-all | bytes 2752512 | tf_op jit(solution)/shard_map/all_to_all | solution.py:30
  176.2 16.0 %fusion.7 = f32[1344,128]{1,0:T(8,128)} fusion(f32[2688,128]{1,0:T(8,128)S(1)} %bitcast.136, f32[1344,1,2688]{2,1,0:T(1,128)} %param.15), kind=kOutput, calls=%fused_computation.16 | convolution fusion | flops 5549064192 | bytes 16515072 | tf_op jit(solution)/shard_map/dot_general | solution.py:123
  192.2 1.3 convolution_bitcast_fusion.3
  193.7 18.3 %all_to_all.42 = f32[16,128,128]{2,1,0:T(8,128)S(1)} all-to-all(f32[16,128,128]{2,1,0:T(8,128)S(1)} %broadcast_in_dim.31), channel_id=1, replica_groups=mesh['row'=16,'col'=8] {'row'}, dimensions={0} | all-to-all | bytes 2097152 | tf_op jit(solution)/shard_map/all_to_all | solution.py:30
  212.0 16.2 %all-gather.7.cloned.1.call-done = f32[10752,128]{1,0:T(8,128)} async-done(((f32[1344,128]{1,0:T(8,128)}), f32[10752,128]{1,0:T(8,128)}) %all-gather.7.cloned.1.call-update) | async-done | bytes 5505040 | tf_op jit(solution)/shard_map/all_gather | solution.py:47
  228.2 2.9 reduce_sum.90
  231.8 1.3 fusion.47
  233.2 1.1 broadcast_in_dim.32
  234.3 6.5 %all-to-all-start.3 = ((f32[16,128,128]{2,1,0:T(8,128)}), f32[16,128,128]{2,1,0:T(8,128)S(1)}, u32[]{:S(2)}, u32[]{:S(2)}) async-start(f32[16,128,128]{2,1,0:T(8,128)} %broadcast_in_dim.32), calls=%async_computation.3 | async-start | bytes 2097152 | tf_op jit(solution)/shard_map/all_to_all | solution.py:30
  240.8 3.6 convolution_bitcast_fusion
  244.4 3.3 copy.52
  247.8 3.6 reshape_reshape.3
  251.4 3.8 pad.4
  255.2 4.3 reshape.74
  259.9 11.7 %cholesky.59 = f32[128,128]{1,0:T(8,128)S(1)} custom-call(f32[128,128]{1,0:T(8,128)S(1)} %fusion.37), custom_call_target="Cholesky" | custom-call | tf_op jit(solution)/shard_map/jit(cholesky)/cholesky | solution.py:70
  273.0 9.8 %custom-call.9 = f32[1,128,128]{1,2,0:T(8,128)S(1)} custom-call(f32[1,128,128]{2,1,0:T(8,128)S(1)} %fusion.17), custom_call_target="InvertDiagBlocksLowerTriangular" | custom-call | tf_op jit(solution)/shard_map/jit(_cho_solve)/triangular_solve | solution.py:71
  284.0 1.3 fusion.49
  285.3 1.1 broadcast_in_dim.33
  286.4 6.7 %all-to-all-start.4 = ((f32[16,128,128]{2,1,0:T(8,128)}), f32[16,128,128]{2,1,0:T(8,128)S(1)}, u32[]{:S(2)}, u32[]{:S(2)}) async-start(f32[16,128,128]{2,1,0:T(8,128)} %broadcast_in_dim.33), calls=%async_computation.4 | async-start | bytes 2097152 | tf_op jit(solution)/shard_map/all_to_all | solution.py:30
  293.5 11.7 %cholesky.70 = f32[128,128]{1,0:T(8,128)S(1)} custom-call(f32[128,128]{1,0:T(8,128)S(1)} %fusion.31), custom_call_target="Cholesky" | custom-call | tf_op jit(solution)/shard_map/jit(cholesky)/cholesky | solution.py:70
  306.5 9.8 %custom-call.10 = f32[1,128,128]{1,2,0:T(8,128)S(1)} custom-call(f32[1,128,128]{2,1,0:T(8,128)S(1)} %fusion.18), custom_call_target="InvertDiagBlocksLowerTriangular" | custom-call | tf_op jit(solution)/shard_map/jit(_cho_solve)/triangular_solve | solution.py:71
  317.8 25.0 %all_to_all.43 = f32[16,168,128]{2,1,0:T(8,128)S(1)} all-to-all(f32[16,168,128]{2,1,0:T(8,128)S(1)} %broadcast_in_dim.34), channel_id=1, replica_groups=mesh['row'=16,'col'=8] {'row'}, dimensions={0} | all-to-all | bytes 2752512 | tf_op jit(solution)/shard_map/all_to_all | solution.py:30
  342.8 16.0 %fusion.10 = f32[1344,128]{1,0:T(8,128)} fusion(f32[2688,128]{1,0:T(8,128)S(1)} %bitcast.137, f32[1344,1,2688]{2,1,0:T(1,128)} %param.15), kind=kOutput, calls=%fused_computation.17 | convolution fusion | flops 5549064192 | bytes 16515072 | tf_op jit(solution)/shard_map/dot_general | solution.py:123
  358.9 108.8 %reduce-scatter.3.cloned.1.call-done = f32[48,128]{1,0:T(8,128)} async-done(((f32[6144,128]{1,0:T(8,128)}), f32[48,128]{1,0:T(8,128)}) %reduce-scatter.3.cloned.1.call-update) | async-done | bytes 24592 | tf_op jit(solution)/shard_map/reduce_scatter | solution.py:24
  467.7 1.3 fusion.42
  469.0 1.3 fusion.50
  470.5 17.1 %all_to_all.44 = f32[16,128,128]{2,1,0:T(8,128)S(1)} all-to-all(f32[16,128,128]{2,1,0:T(8,128)S(1)} %broadcast_in_dim.35), channel_id=1, replica_groups=mesh['row'=16,'col'=8] {'row'}, dimensions={0} | all-to-all | bytes 2097152 | tf_op jit(solution)/shard_map/all_to_all | solution.py:30
  487.7 19.0 %all-gather.9.cloned.1.call-done = f32[10752,128]{1,0:T(8,128)} async-done(((f32[1344,128]{1,0:T(8,128)}), f32[10752,128]{1,0:T(8,128)}) %all-gather.9.cloned.1.call-update) | async-done | bytes 5505040 | tf_op jit(solution)/shard_map/all_gather | solution.py:47
  506.7 2.9 reduce_sum.94
  509.6 0.7 convolution_add_fusion
  510.4 1.4 fusion.51
  511.7 1.1 broadcast_in_dim.36
  512.8 6.7 %all-to-all-start.7 = ((f32[16,128,128]{2,1,0:T(8,128)}), f32[16,128,128]{2,1,0:T(8,128)S(1)}, u32[]{:S(2)}, u32[]{:S(2)}) async-start(f32[16,128,128]{2,1,0:T(8,128)} %broadcast_in_dim.36), calls=%async_computation.7 | async-start | bytes 2097152 | tf_op jit(solution)/shard_map/all_to_all | solution.py:30
  519.5 61.4 %all-gather.11.cloned.1.call-done = f32[128,42,128]{2,1,0:T(8,128)} async-done(((f32[1,42,128]{2,1,0:T(8,128)}), f32[128,42,128]{2,1,0:T(8,128)}) %all-gather.11.cloned.1.call-update) | async-done | bytes 2752528 | tf_op jit(solution)/shard_map/all_gather | solution.py:142
  580.9 4.1 reshape.79
  586.0 11.7 %cholesky.81 = f32[128,128]{1,0:T(8,128)S(1)} custom-call(f32[128,128]{1,0:T(8,128)S(1)} %fusion.24), custom_call_target="Cholesky" | custom-call | tf_op jit(solution)/shard_map/jit(cholesky)/cholesky | solution.py:70
  599.1 9.8 %custom-call.11 = f32[1,128,128]{1,2,0:T(8,128)S(1)} custom-call(f32[1,128,128]{2,1,0:T(8,128)S(1)} %fusion.19), custom_call_target="InvertDiagBlocksLowerTriangular" | custom-call | tf_op jit(solution)/shard_map/jit(_cho_solve)/triangular_solve | solution.py:71
  610.1 6.0 fusion.6
  (82 shorter events, 13.5 us)
Async XLA Ops:
  6.5 2.8 copy-start
  6.5 126.3 %all-reduce.4.cloned.1.call-start = ((), (), s32[]{:S(2)}) async-start(), calls=%async_computation.13 | async-start | bytes 11010048
  9.4 1.5 copy-start.2
  14.5 0.7 copy-start.8
  135.7 16.3 %all-to-all-start = ((f32[8,168,128]{2,1,0:T(8,128)}), f32[8,168,128]{2,1,0:T(8,128)S(1)}, u32[]{:S(2)}, u32[]{:S(2)}) async-start(f32[8,168,128]{2,1,0:T(8,128)} %broadcast_in_dim.28), calls=%async_computation | async-start | bytes 1376256 | tf_op jit(solution)/shard_map/all_to_all | solution.py:30
  140.8 87.5 %all-gather.7.cloned.1.call-start = ((), (), s32[]{:S(2)}) async-start(), calls=%async_computation.10 | async-start | bytes 6193152 | tf_op jit(solution)/shard_map/all_gather | solution.py:47
  234.3 25.4 %all-to-all-start.3 = ((f32[16,128,128]{2,1,0:T(8,128)}), f32[16,128,128]{2,1,0:T(8,128)S(1)}, u32[]{:S(2)}, u32[]{:S(2)}) async-start(f32[16,128,128]{2,1,0:T(8,128)} %broadcast_in_dim.32), calls=%async_computation.3 | async-start | bytes 2097152 | tf_op jit(solution)/shard_map/all_to_all | solution.py:30
  240.8 226.9 %reduce-scatter.3.cloned.1.call-start = ((), (), s32[]{:S(2)}) async-start(), calls=%async_computation.9 | async-start | bytes 3170304 | tf_op jit(solution)/shard_map/reduce_scatter | solution.py:24
  283.3 3.1 copy-start.3
  286.4 29.9 %all-to-all-start.4 = ((f32[16,128,128]{2,1,0:T(8,128)}), f32[16,128,128]{2,1,0:T(8,128)S(1)}, u32[]{:S(2)}, u32[]{:S(2)}) async-start(f32[16,128,128]{2,1,0:T(8,128)} %broadcast_in_dim.33), calls=%async_computation.4 | async-start | bytes 2097152 | tf_op jit(solution)/shard_map/all_to_all | solution.py:30
  293.1 213.6 %all-gather.9.cloned.1.call-start = ((), (), s32[]{:S(2)}) async-start(), calls=%async_computation.11 | async-start | bytes 6193152 | tf_op jit(solution)/shard_map/all_gather | solution.py:47
  316.5 26.3 %copy-start.5 = (f32[128,128]{0,1:T(8,128)}, f32[128,128]{0,1:T(8,128)S(1)}, u32[]{:S(2)}) copy-start(f32[128,128]{0,1:T(8,128)S(1)} %copy.49) | copy-start | bytes 196612
  342.8 124.9 %copy-start.7 = (f32[42,128]{1,0:T(8,128)S(1)}, f32[42,128]{1,0:T(8,128)}, u32[]{:S(2)}) copy-start(f32[42,128]{1,0:T(8,128)} %param.16) | copy-start | bytes 64516
  358.9 222.1 %all-gather.11.cloned.1.call-start = ((), (), s32[]{:S(2)}) async-start(), calls=%async_computation.12 | async-start | bytes 3170304 | tf_op jit(solution)/shard_map/all_gather | solution.py:142
  512.8 72.9 %all-to-all-start.7 = ((f32[16,128,128]{2,1,0:T(8,128)}), f32[16,128,128]{2,1,0:T(8,128)S(1)}, u32[]{:S(2)}, u32[]{:S(2)}) async-start(f32[16,128,128]{2,1,0:T(8,128)} %broadcast_in_dim.36), calls=%async_computation.7 | async-start | bytes 2097152 | tf_op jit(solution)/shard_map/all_to_all | solution.py:30
  519.5 65.5 %copy-start.4 = (f32[128,128]{1,0:T(8,128)S(1)}, f32[128,128]{1,0:T(8,128)}, u32[]{:S(2)}) copy-start(f32[128,128]{1,0:T(8,128)} %copy-done.3) | copy-start | bytes 196612
  585.0 23.9 %copy-start.6 = (f32[128,128]{0,1:T(8,128)S(1)}, f32[128,128]{0,1:T(8,128)}, u32[]{:S(2)}) copy-start(f32[128,128]{0,1:T(8,128)} %copy-done.5) | copy-start | bytes 196612
  609.2 7.0 %copy-start.1 = (bf16[336,1,2688]{2,0,1:T(8,128)(2,1)S(1)}, bf16[336,1,2688]{2,0,1:T(8,128)(2,1)}, u32[]{:S(2)}) copy-start(bf16[336,1,2688]{2,0,1:T(8,128)(2,1)} %param.13) | copy-start | bytes 5419012
Sparse Core Ops, SparseCore 0:
  14.7 118.1 all-reduce.3
  192.4 35.8 all-gather.6
  259.6 208.0 reduce-scatter.2
  469.2 37.4 all-gather.8
  509.6 71.3 all-gather.10
where the time goes:
time: 631 us; the launch traced here: 623 us
  waiting for transfers between devices  333 us (53%)
  blocking collectives  84.5 us (13%)
  other arithmetic  83 us (13%)
  matrix products  55.8 us (9%)
  local copies, waits for them, and re-layouts  26.7 us (4%)
  starting transfers between devices  25.3 us (4%)
  between operations  14.5 us (2%)
    unnamed x6, waiting for transfers between devices  117 us
    reduce_scatter x1, waiting for transfers between devices, own_tiles(): own = lax.psum_scatter(lines, axis, scatter_dimension=0, tiled=True)  109 us
    all_to_all x4, blocking collectives, copy_for_each(): lax.all_to_all(jnp.broadcast_to(array[None], (peers, *array.shape)), axis...  84.5 us
    all_gather x1, waiting for transfers between devices, body(): lax.all_gather(residual_t, ('row', 'col'), axis=0, tiled=True)  61.4 us
    another operation x9, other arithmetic, small_solve(): factor = jnp.linalg.cholesky(matrix)  37.2 us
    all_gather x2, waiting for transfers between devices, gathered_total(): tiles = lax.all_gather(array, axis)  35.2 us
    dot_general x2, matrix products, body(): jnp.dot(cov_flat, gathered_copies(own_piece(direction), 'row', 0), precis...  32 us
    another operation x6, other arithmetic, small_solve(): return jax.scipy.linalg.cho_solve((factor, True), right)  31.4 us
  transfers between devices with their start and end apart: 9, of which 6 were waited for; matrix products, arithmetic and copies ran while one was open for 16% of the time, Pallas kernels for 0%

commit v1 on v0

v1 whole, which is shorter than its diff:
```python
import math

import jax
import jax.numpy as jnp
from jax import lax
from jax.experimental import pallas as pl
from jax.experimental.pallas import tpu as pltpu
from jax.sharding import PartitionSpec as P

FF = 21504
D = 5376
PIECE = 168
E = 128
F32 = jnp.float32
BF16 = jnp.bfloat16
HI = lax.Precision.HIGHEST
N_SEM = 112
COV_ROWS = 112
COV_STEPS = 1344 // COV_ROWS
LINES = COV_ROWS * 21


def dot(left, right):
    return lax.dot_general(left, right, (((1,), (0,)), ((), ())), precision=HI, preferred_element_type=F32)


def dot_t(left, right):
    return lax.dot_general(left, right, (((0,), (0,)), ((), ())), precision=HI, preferred_element_type=F32)


def dot_b(left, right):
    return lax.dot_general(left, right, (((1,), (0,)), ((), ())), preferred_element_type=F32)


def dot_tb(left, right):
    return lax.dot_general(left, right, (((0,), (0,)), ((), ())), preferred_element_type=F32)


def halves(value):
    high = value.astype(BF16)
    return high, (value - high.astype(F32)).astype(BF16)


def sym(matrix):
    return 0.5 * (matrix + matrix.T)


def sweep_panel(matrix):
    lane = lax.broadcasted_iota(jnp.int32, (E, E), 1)
    sub = lax.broadcasted_iota(jnp.int32, (E, E), 0)
    lane1 = lax.broadcasted_iota(jnp.int32, (1, E), 1)
    for j in range(8):
        column = matrix[:, j : j + 1]
        row = matrix[j : j + 1, :]
        inv = 1.0 / matrix[j : j + 1, j : j + 1]
        row = jnp.where(lane1 == j, inv, row * inv)
        rest = jnp.where(lane == j, 0.0, matrix) - column * row
        matrix = jnp.where(sub == j, row, rest)
    matrix = jnp.concatenate([matrix[8:], matrix[:8]], axis=0)
    return pltpu.roll(matrix, E - 8, 1)


def sweep_some(count, *matrices):
    return lax.fori_loop(0, count, lambda _, ms: tuple(sweep_panel(m) for m in ms), matrices)


def kernel(
    states_h, pos, gw_h, uw_h, dw_h, cov_h, tgt,
    out,
    states, gw, uw, dw, cbuf, flat, gate, up, ra1, rb1, rc1, ra2, rb2, rc2,
    chi, clo, piece, bc, wc, bhl, whl, vv, vk, va, vb, vc, wr,
    part, rk, pa, pb, pc, xr, yr, res, tp, m0, n12, n3, send, recv, local,
):
    a = lax.axis_index("row")
    b = lax.axis_index("col")
    x, y = a // 4, a % 4
    z, k = b // 2, b % 2

    def dev_x(d):
        return {"row": ((x + d) % 4) * 4 + y}

    def dev_y(d):
        return {"row": x * 4 + (y + d) % 4}

    def dev_z(d):
        return {"col": ((z + d) % 4) * 2 + k}

    dev_k = {"col": z * 2 + 1 - k}
    sent = []

    def cp(src, dst, sem, dev):
        copy = pltpu.make_async_remote_copy(
            src_ref=src, dst_ref=dst, send_sem=send.at[sem], recv_sem=recv.at[sem],
            device_id=dev, device_id_type=pl.DeviceIdType.MESH,
        )
        copy.start()
        sent.append(copy)
        return copy

    loads = [
        pltpu.make_async_copy(src, dst, local.at[i])
        for i, (src, dst) in enumerate(((states_h, states), (gw_h, gw), (uw_h, uw), (dw_h, dw)))
    ]
    for load in loads:
        load.start()

    def cov_load(step, slot):
        return pltpu.make_async_copy(
            cov_h.at[pl.ds(pl.multiple_of(step * LINES, 8), LINES)], cbuf.at[slot], local.at[4 + slot]
        )

    cov_load(0, 0).start()

    barrier = pltpu.get_barrier_semaphore()
    peers = [dev(d) for dev in (dev_x, dev_y, dev_z) for d in (1, 2, 3)] + [dev_k]
    for peer in peers:
        pl.semaphore_signal(barrier, inc=1, device_id=peer, device_id_type=pl.DeviceIdType.MESH)
    pl.semaphore_wait(barrier, len(peers))

    def ring_start(data, ra, rb, me, dev, sem):
        m1, m2, m3 = (me + 1) % 4, (me + 2) % 4, (me + 3) % 4
        return [
            cp(data(0, m2), ra(0), sem, dev(1)),
            cp(data(1, m2), ra(1), sem + 1, dev(3)),
            cp(data(0, m3), rb(0), sem + 2, dev(3)),
            cp(data(1, m1), rb(1), sem + 3, dev(1)),
        ]

    def ring_middle(copies, data, ra, rc, me, dev, sem):
        m1, m3 = (me + 1) % 4, (me + 3) % 4
        copies[0].wait_recv()
        data(0, m1)[...] += ra(0)[...]
        c0 = cp(data(0, m1), rc(0), sem + 4, dev(1))
        copies[1].wait_recv()
        data(1, m3)[...] += ra(1)[...]
        c1 = cp(data(1, m3), rc(1), sem + 5, dev(3))
        return [copies[2], copies[3], c0, c1]

    def ring_end(copies, data, rb, rc, me):
        for copy in copies:
            copy.wait_recv()
        for h in (0, 1):
            data(h, me)[...] += rb(h)[...] + rc(h)[...]

    loads[0].wait()
    tokens = []
    for p in (0, 1):
        where = pos[p : p + 1, :]
        chosen = jnp.zeros((336, E), F32)
        for s in range(8):
            chosen = jnp.where(where == s, states[p, s].astype(F32), chosen)
        tokens.append(chosen.astype(BF16))
    tokens = jnp.concatenate(tokens, axis=1)

    def project(weight, target, by_y):
        def chunk(j, carry):
            at = pl.multiple_of(j * 384, 128)
            flat[pl.ds(at, 384), :] = dot_tb(weight[:, pl.ds(at, 384)], tokens)
            return carry

        lax.fori_loop(0, 7, chunk, 0)

        def place(i, carry):
            px, py = i // 4, i % 4
            first, second = (py, px) if by_y else (px, py)
            at = pl.multiple_of(i * PIECE, 8)
            for p in (0, 1):
                target[p, first, second] = flat[pl.ds(at, PIECE), p * E : (p + 1) * E]
            return carry

        lax.fori_loop(0, 16, place, 0)

    def gate_data(h, t):
        return gate.at[h, t]

    def up_data(h, t):
        return up.at[h, t]

    def gate_data2(h, t):
        return gate.at[h, x, t]

    def up_data2(h, t):
        return up.at[h, y, t]

    def buf(ref, which):
        return lambda h: ref.at[which, h]

    loads[1].wait()
    project(gw, gate, False)
    g1 = ring_start(gate_data, buf(ra1, 0), buf(rb1, 0), x, dev_x, 0)
    loads[2].wait()
    project(uw, up, True)
    u1 = ring_start(up_data, buf(ra1, 1), buf(rb1, 1), y, dev_y, 6)

    def cov_step(step, carry):
        slot = step % 2

        @pl.when(step + 1 < COV_STEPS)
        def _():
            cov_load(step + 1, 1 - slot).start()

        cov_load(step, slot).wait()
        rows = pl.ds(pl.multiple_of(step * COV_ROWS, 16), COV_ROWS)
        for t in range(21):
            high, low = halves(cbuf[slot, pl.ds(t, COV_ROWS, stride=21), :])
            chi[rows, t * E : (t + 1) * E] = high
            clo[rows, t * E : (t + 1) * E] = low
        return carry

    lax.fori_loop(0, COV_STEPS // 2, cov_step, 0)
    g1 = ring_middle(g1, gate_data, buf(ra1, 0), buf(rc1, 0), x, dev_x, 0)
    u1 = ring_middle(u1, up_data, buf(ra1, 1), buf(rc1, 1), y, dev_y, 6)
    lax.fori_loop(COV_STEPS // 2, COV_STEPS, cov_step, 0)
    ring_end(g1, gate_data, buf(rb1, 0), buf(rc1, 0), x)
    g2 = ring_start(gate_data2, buf(ra2, 0), buf(rb2, 0), y, dev_y, 12)
    ring_end(u1, up_data, buf(rb1, 1), buf(rc1, 1), y)
    u2 = ring_start(up_data2, buf(ra2, 1), buf(rb2, 1), x, dev_x, 18)
    g2 = ring_middle(g2, gate_data2, buf(ra2, 0), buf(rc2, 0), y, dev_y, 12)
    u2 = ring_middle(u2, up_data2, buf(ra2, 1), buf(rc2, 1), x, dev_x, 18)
    ring_end(g2, gate_data2, buf(rb2, 0), buf(rc2, 0), y)
    ring_end(u2, up_data2, buf(rb2, 1), buf(rc2, 1), x)

    keys = jnp.zeros((PIECE, E), F32)
    for p in (0, 1):
        v = gate[p, x, y]
        keys = keys + v / (1.0 + jnp.exp(-v)) * up[p, y, x]
    keys = keys * 0.5
    keys_half = keys.astype(BF16)
    piece[0] = 4.0 / math.sqrt(FF) * keys
    top, low = pl.ds(0, 88), pl.ds(88, 80)

    def gather_start(field, own, sem):
        field[x, y] = piece[own]
        return [cp(field.at[x, y, top], field.at[x, y, top], sem + d - 1, dev_x(d)) for d in (1, 2, 3)] + [
            cp(field.at[x, y, low], field.at[x, y, low], sem + 2 + d, dev_y(d)) for d in (1, 2, 3)
        ]

    def gather_middle(copies, field, sem):
        for copy in copies[:3]:
            copy.wait_recv()
        mine = field.at[:, y, top]
        out_y = [cp(mine, mine, sem + 6, dev_y(1)), cp(mine, mine, sem + 7, dev_y(3))]
        for copy in copies[3:]:
            copy.wait_recv()
        mine = field.at[x, :, low]
        out_x = [cp(mine, mine, sem + 8, dev_x(1)), cp(mine, mine, sem + 9, dev_x(3))]
        return out_y + out_x

    def gather_forward(copies, field, sem):
        y1, y3, x1, x3 = (y + 1) % 4, (y + 3) % 4, (x + 1) % 4, (x + 3) % 4
        copies[0].wait_recv()
        part0 = field.at[:, y3, pl.ds(0, 48)]
        f0 = cp(part0, part0, sem + 10, dev_y(1))
        copies[1].wait_recv()
        part1 = field.at[:, y1, pl.ds(48, 40)]
        f1 = cp(part1, part1, sem + 11, dev_y(3))
        copies[2].wait_recv()
        part2 = field.at[x3, :, pl.ds(88, 40)]
        f2 = cp(part2, part2, sem + 12, dev_x(1))
        copies[3].wait_recv()
        part3 = field.at[x1, :, pl.ds(128, 40)]
        f3 = cp(part3, part3, sem + 13, dev_x(3))
        return [f0, f1, f2, f3]

    def split_field(field, target):
        def body(i, carry):
            rows = pl.ds(pl.multiple_of(i * 336, 16), 336)
            high, rest = halves(field[i // 2, pl.ds((i % 2) * 2, 2)].reshape(336, E))
            target[rows, :E] = high
            target[rows, E:] = rest
            return carry

        lax.fori_loop(0, 8, body, 0)

    def gram(left, right):
        def body(i, total):
            rows = pl.ds(pl.multiple_of(i * 336, 16), 336)
            return total + dot_tb(left[rows, :], right[rows, :])

        total = lax.fori_loop(0, 8, body, jnp.zeros((2 * E, 2 * E), F32))
        return (total[:E, :E] + total[E:, E:]) + (total[:E, E:] + total[E:, :E])

    def cov_times(i, target):
        rows = pl.ds(pl.multiple_of(i * 336, 16), 336)
        both = dot_b(chi[rows, :], target[...])
        return both[:, :E] + (both[:, E:] + dot_b(clo[rows, :], target[:, :E]))

    bg = gather_start(bc, 0, 24)

    loads[3].wait()
    tp[...] = jnp.zeros_like(tp)
    tp[0:42, :] = tgt[...]
    first = (a * 8 + b) * 42

    def current(j, carry):
        at = pl.multiple_of(j * 384, 128)
        value = dot_tb(keys_half, dw[:, pl.ds(at, 384)])
        place = lax.broadcasted_iota(jnp.int32, (48, 384), 1) + j * 384 - first
        mark = jnp.where(place == lax.broadcasted_iota(jnp.int32, (48, 384), 0), 1.0, 0.0)
        value = dot_t(tp[...], mark) - value
        for i in range(3):
            part[j * 3 + i] = value[:, i * E : (i + 1) * E]
        return carry

    lax.fori_loop(0, 14, current, 0)
    for i in range(42, 48):
        part[i] = jnp.zeros((E, E), F32)
    real = pl.ds(0, 42)

    def half_of(kk):
        return pl.ds(pl.multiple_of(kk * 64, 8), 64)

    p1 = cp(part.at[real, half_of(1 - k)], rk, 52, dev_k)
    bg = gather_middle(bg, bc, 24)

    def part_data(h, t):
        return part.at[real, pl.ds(pl.multiple_of(k * 64 + t * 16 + h * 8, 8), 8)]

    p1.wait_recv()

    def add_half(i, carry):
        part[i, half_of(k), :] += rk[i]
        return carry

    lax.fori_loop(0, 42, add_half, 0)
    bf = gather_forward(bg, bc, 24)
    pz = ring_start(part_data, lambda h: pa.at[h], lambda h: pb.at[h], z, dev_z, 53)
    for copy in bf:
        copy.wait_recv()
    split_field(bc, bhl)
    m0[0] = gram(bhl, bhl)
    mk = cp(m0.at[0], m0.at[1], 59, dev_k)

    def first_image(i, carry):
        value = cov_times(i, bhl)
        vv[i, 0] = value[:PIECE]
        vv[i, 1] = value[PIECE:]
        return carry

    lax.fori_loop(0, 4, first_image, 0)
    v1 = cp(vv.at[:, 1 - k], vk, 60, dev_k)
    pz = ring_middle(pz, part_data, lambda h: pa.at[h], lambda h: pc.at[h], z, dev_z, 53)
    v1.wait_recv()
    vv[:, k] += vk[...]

    def image_data(h, t):
        return vv.at[t, k, top if h == 0 else low]

    def image_buf(ref):
        return lambda h: ref.at[h, pl.ds(0, 88 if h == 0 else 80)]

    vz = ring_start(image_data, image_buf(va), image_buf(vb), z, dev_z, 61)
    mk.wait_recv()
    m0[2] = m0[0] + m0[1]
    vz = ring_middle(vz, image_data, image_buf(va), image_buf(vc), z, dev_z, 61)
    mz = [cp(m0.at[2], m0.at[2 + d], 66 + d, dev_z(d)) for d in (1, 2, 3)]
    ring_end(vz, image_data, image_buf(vb), image_buf(vc), z)
    piece[1] = vv[z, k]
    wg = gather_start(wc, 1, 38)
    wr[z, k] = piece[1]
    wz = [cp(wr.at[z, k], wr.at[z, k], 69 + d, dev_z(d)) for d in (1, 2, 3)]
    ring_end(pz, part_data, lambda h: pb.at[h], lambda h: pc.at[h], z)
    wg = gather_middle(wg, wc, 38)
    wf = gather_forward(wg, wc, 38)
    own_rows = pl.ds(pl.multiple_of(k * 64 + z * 16, 8), 16)

    def twelve(t):
        return pl.ds(t * 12, 12)

    px = [cp(part.at[twelve((x + d) % 4), own_rows], xr.at[d - 1], 72 + d, dev_x(d)) for d in (1, 2, 3)]
    for copy in wz:
        copy.wait_recv()
    wk = cp(wr.at[:, k], wr.at[:, k], 76, dev_k)
    for copy in mz:
        copy.wait_recv()
    gram0 = sym((m0[2] + m0[3]) + (m0[4] + m0[5]))
    for copy in wf:
        copy.wait_recv()
    split_field(wc, whl)
    n12[0, 0] = gram(bhl, whl)
    n12[0, 1] = gram(whl, whl)
    nk = cp(n12.at[0], n12.at[1], 77, dev_k)
    wk.wait_recv()

    def second_image(i, total):
        value = cov_times(i, whl)
        return total + dot_t(wr[i].reshape(336, E), value)

    n3[0] = lax.fori_loop(0, 4, second_image, jnp.zeros((E, E), F32))
    n3k = cp(n3.at[0], n3.at[1], 78, dev_k)
    nk.wait_recv()
    n12[2] = n12[0] + n12[1]
    nz = [cp(n12.at[2], n12.at[2 + d], 78 + d, dev_z(d)) for d in (1, 2, 3)]
    n3k.wait_recv()
    n3[2] = n3[0] + n3[1]
    n3z = [cp(n3.at[2], n3.at[2 + d], 81 + d, dev_z(d)) for d in (1, 2, 3)]

    for copy in px:
        copy.wait_recv()
    part[twelve(x), own_rows] += (xr[0] + xr[1]) + xr[2]

    def three(t):
        return pl.ds(x * 12 + t * 3, 3)

    py = [cp(part.at[three((y + d) % 4), own_rows], yr.at[d - 1], 84 + d, dev_y(d)) for d in (1, 2, 3)]
    for copy in nz:
        copy.wait_recv()
    both = (n12[2] + n12[3]) + (n12[4] + n12[5])
    n1, n2 = sym(both[0]), both[1]
    square = dot(gram0, gram0)
    m1 = sym(n1 + square)
    n1m0 = dot(n1, gram0)
    m2 = sym(n2 + n1m0 + n1m0.T + dot(square, gram0))
    n2m0 = dot(n2, gram0)
    m3_rest = sym(n2m0 + n2m0.T + dot(gram0, n1m0) + dot(m1, m1))
    for copy in n3z:
        copy.wait_recv()
    n3[6] = (n3[2] + n3[3]) + (n3[4] + n3[5])
    n3y = [cp(n3.at[6], n3.at[6 + d], 87 + d, dev_y(d)) for d in (1, 2, 3)]
    for copy in py:
        copy.wait_recv()
    res[three(y), own_rows] = part[three(y), own_rows] + ((yr[0] + yr[1]) + yr[2])
    mine = res.at[three(y), own_rows]
    ry = [cp(mine, mine, 90 + d, dev_y(d)) for d in (1, 2, 3)]
    inv0, inv1 = sweep_some(4, gram0, m1)
    for copy in n3y:
        copy.wait_recv()
    n3[10] = (n3[6] + n3[7]) + (n3[8] + n3[9])
    n3x = [cp(n3.at[10], n3.at[10 + d], 93 + d, dev_x(d)) for d in (1, 2, 3)]
    for copy in ry:
        copy.wait_recv()
    mine_x = res.at[twelve(x), own_rows]
    rx = [cp(mine_x, mine_x, 96 + d, dev_x(d)) for d in (1, 2, 3)]
    inv0, inv1 = sweep_some(6, inv0, inv1)
    for copy in rx:
        copy.wait_recv()
    mine_z = res.at[real, own_rows]
    rz = [cp(mine_z, mine_z, 100, dev_z(1)), cp(mine_z, mine_z, 101, dev_z(3))]
    inv0, inv1 = sweep_some(6, inv0, inv1)

    def rows_of(zz, h):
        return pl.ds(pl.multiple_of(k * 64 + zz * 16 + h * 8, 8), 8)

    rz[0].wait_recv()
    fwd0 = res.at[real, rows_of((z + 3) % 4, 0)]
    rf0 = cp(fwd0, fwd0, 102, dev_z(1))
    rz[1].wait_recv()
    fwd1 = res.at[real, rows_of((z + 1) % 4, 1)]
    rf1 = cp(fwd1, fwd1, 103, dev_z(3))
    alpha0 = dot(inv1, gram0)
    norm1 = sym(dot_t(alpha0, dot(m2, alpha0)) - gram0)
    beta = dot(inv0, norm1)
    eye = jnp.where(
        lax.broadcasted_iota(jnp.int32, (E, E), 0) == lax.broadcasted_iota(jnp.int32, (E, E), 1), 1.0, 0.0
    )
    c1 = eye + beta
    cross = dot_t(c1, dot(m2, alpha0))
    curv_rest = dot_t(c1, dot(m1, c1)) - cross - cross.T
    for copy in n3x:
        copy.wait_recv()
    m3 = m3_rest + sym((n3[10] + n3[11]) + (n3[12] + n3[13]))
    curvature = sym(curv_rest + dot_t(alpha0, dot(m3, alpha0)))
    (inv2,) = sweep_some(16, curvature)
    rf0.wait_recv()
    rf1.wait_recv()
    half = res.at[real, half_of(k)]
    rkk = cp(half, half, 104, dev_k)
    alpha1 = dot(inv2, norm1)
    on_w = -dot(alpha0, alpha1)
    m0[3] = dot(c1, alpha1)
    m0[4] = dot(gram0, on_w)
    on_b = alpha0 + (m0[3] + m0[4])
    fh, fl = halves(jnp.concatenate([piece[0], piece[1]], axis=1))
    ch, cl = halves(jnp.concatenate([on_b, on_w], axis=0))
    found = dot_b(fh, ch) + (dot_b(fh, cl) + dot_b(fl, ch))
    xh, xl = halves(found)
    xhh = jnp.concatenate([xh, xh], axis=1)
    rkk.wait_recv()

    def update(j, carry):
        right = jnp.concatenate([res[j * 2], res[j * 2 + 1]], axis=1)
        rh, rl = halves(right)
        value = dot_b(xhh, jnp.concatenate([rh, rl], axis=0)) + dot_b(xl, rh)
        out[:, pl.ds(pl.multiple_of(j * 256, 128), 256)] = value.astype(BF16)
        return carry

    lax.fori_loop(0, 21, update, 0)
    for copy in sent:
        copy.wait_send()


def body(states, subject_pos, gate_weight, up_weight, down_weight, covariance, targets):
    vmem = pl.BlockSpec(memory_space=pltpu.VMEM)
    anyw = pl.BlockSpec(memory_space=pl.ANY)
    small = lambda *dims: pltpu.VMEM(dims, F32)
    update = pl.pallas_call(
        kernel,
        out_shape=jax.ShapeDtypeStruct((PIECE, D), BF16),
        in_specs=[anyw, vmem, anyw, anyw, anyw, anyw, vmem],
        out_specs=vmem,
        scratch_shapes=[
            pltpu.VMEM((2, 8, 336, E), BF16),
            pltpu.VMEM((336, 2688), BF16),
            pltpu.VMEM((336, 2688), BF16),
            pltpu.VMEM((PIECE, D), BF16),
            small(2, LINES, E),
            small(2688, 2 * E),
            small(2, 4, 4, PIECE, E),
            small(2, 4, 4, PIECE, E),
            small(2, 2, 4, PIECE, E),
            small(2, 2, 4, PIECE, E),
            small(2, 2, 4, PIECE, E),
            small(2, 2, PIECE, E),
            small(2, 2, PIECE, E),
            small(2, 2, PIECE, E),
            pltpu.VMEM((1344, 2688), BF16),
            pltpu.VMEM((1344, 2688), BF16),
            small(2, PIECE, E),
            small(4, 4, PIECE, E),
            small(4, 4, PIECE, E),
            pltpu.VMEM((2688, 2 * E), BF16),
            pltpu.VMEM((2688, 2 * E), BF16),
            small(4, 2, PIECE, E),
            small(4, PIECE, E),
            small(2, 88, E),
            small(2, 88, E),
            small(2, 88, E),
            small(4, 2, PIECE, E),
            small(48, E, E),
            small(42, 64, E),
            small(2, 42, 8, E),
            small(2, 42, 8, E),
            small(2, 42, 8, E),
            small(3, 12, 16, E),
            small(3, 3, 16, E),
            small(48, E, E),
            small(48, E),
            small(6, E, E),
            small(6, 2, E, E),
            small(14, E, E),
            pltpu.SemaphoreType.DMA((N_SEM,)),
            pltpu.SemaphoreType.DMA((N_SEM,)),
            pltpu.SemaphoreType.DMA((6,)),
        ],
        compiler_params=pltpu.CompilerParams(
            collective_id=0, has_side_effects=True, vmem_limit_bytes=60 * 1024 * 1024
        ),
        name="edit",
    )(
        jnp.transpose(states, (1, 2, 3, 0)),
        subject_pos.T,
        gate_weight.reshape(336, 2688),
        up_weight.reshape(336, 2688),
        down_weight.reshape(PIECE, D),
        covariance.reshape(1344 * 21, E),
        targets,
    )
    return update.reshape(1, 1, PIECE, D)


def solution(mesh):
    return jax.shard_map(
        body,
        mesh=mesh,
        in_specs=(
            P(None, None, None, "row"),
            P(),
            P("row", "col", None),
            P("row", "col", None),
            P("row", "col", None, None),
            P("row", "col", None),
            P(("row", "col"), None),
        ),
        out_specs=P("row", "col", None, None),
        check_vma=False,
    )
```

time: 631 us -> 165 us (0.26); the launches traced: 623 us -> 164 us
  waiting for transfers between devices: 333 us -> 0 us
  Pallas kernels: 0 us -> 161 us
  blocking collectives: 84.5 us -> 0 us
  other arithmetic: 83 us -> 0 us
  matrix products: 55.8 us -> 0 us
  starting transfers between devices: 25.3 us -> 0 us
  local copies, waits for them, and re-layouts: 26.7 us -> 2.83 us
  between operations: 14.5 us -> 0.01 us
    pallas_call x0 -> x1, Pallas kernels: none -> 161 us  [body(): pl.pallas_call(kernel, out_shape=jax.ShapeDtypeStruct((PIECE, D), BF16),...]
    unnamed x6 -> x0, waiting for transfers between devices: 117 us -> none
    reduce_scatter x1 -> x0, waiting for transfers between devices: 109 us -> none  [own_tiles(): own = lax.psum_scatter(lines, axis, scatter_dimension=0, tiled=True)]
    all_gather x3 -> x0, waiting for transfers between devices: 96.7 us -> none  [the longest x1 61.4 us: body(): lax.all_gather(residual_t, ('row', 'col'), axis=0, tiled=True)]
    all_to_all x4 -> x0, blocking collectives: 84.5 us -> none  [copy_for_each(): lax.all_to_all(jnp.broadcast_to(array[None], (peers, *array.shape)), axis...]
    another operation x15 -> x0, other arithmetic: 68.6 us -> none  [the longest x9 37.2 us: small_solve(): factor = jnp.linalg.cholesky(matrix)]
    dot_general x17 -> x0, matrix products: 54.3 us -> none  [the longest x2 32 us: body(): jnp.dot(cov_flat, gathered_copies(own_piece(direction), 'row', 0), precis...]
    all_to_all x4 -> x0, starting transfers between devices: 25 us -> none  [copy_for_each(): lax.all_to_all(jnp.broadcast_to(array[None], (peers, *array.shape)), axis...]
  transfers between devices with their start and end apart: 9 -> 0, of which waited for: 6 -> 0; matrix products, arithmetic and copies ran while one was open for 16% -> 0% of each run, Pallas kernels for 0% -> 0%
where the time goes in v1:
time: 165 us; the launch traced here: 164 us
  Pallas kernels  161 us (98%)
  local copies, waits for them, and re-layouts  2.83 us (2%)
    pallas_call x1, Pallas kernels, body(): pl.pallas_call(kernel, out_shape=jax.ShapeDtypeStruct((PIECE, D), BF16),...  161 us

profile of v1, /device:TPU:1, one launch (start us, length us, event | category | flops | bytes accessed | tf_op | source)
XLA Modules:
  0.0 164.0 jit_solution(7830731899329868500)
XLA Ops:
  0.0 161.2 %edit.1 = bf16[168,5376]{1,0:T(8,128)(2,1)} custom-call(bf16[2,8,336,128]{3,2,1,0:T(8,128)(2,1)} %bitcast.12, s32[2,128]{1,0:T(2,128)} %bitcast.13, bf16[336,2688]{1,0:T(8,128)(2,1)} %bitcast.9, bf16[336,2688]{1,0:T(8,128)(2,1)} %bitcast.10, bf16[168,5376]{1,0:T(8,128)(2,1)} %bitcast.11, f32[28224,128]{1,0:T(8,128)} %bitcast.7, f32[42,128]{1,0:T(8,128)} %tgt.1), custom_call_target="tpu_custom_call" | custom-call | tf_op jit(solution)/shard_map/edit/pallas_call | solution.py:496
  161.2 2.8 %copy.9 = bf16[1,1,168,5376]{3,2,1,0:T(8,128)(2,1)} copy(bf16[1,1,168,5376]{3,2,1,0:T(8,128)(2,1)} %bitcast.8) | data formatting | bytes 3612672

commit v2 on v1

--- a/solution.py
+++ b/solution.py
@@ -14,7 +14,7 @@
 F32 = jnp.float32
 BF16 = jnp.bfloat16
 HI = lax.Precision.HIGHEST
-N_SEM = 112
+N_SEM = 132
 COV_ROWS = 112
 COV_STEPS = 1344 // COV_ROWS
 LINES = COV_ROWS * 21
@@ -69,7 +69,7 @@
     out,
     states, gw, uw, dw, cbuf, flat, gate, up, ra1, rb1, rc1, ra2, rb2, rc2,
     chi, clo, piece, bc, wc, bhl, whl, vv, vk, va, vb, vc, wr,
-    part, rk, pa, pb, pc, xr, yr, res, tp, m0, n12, n3, send, recv, local,
+    part, rk, pa, pb, pc, xr, yr, res, tp, m0, n12, n3, mc, nc, mc2, mzr, nzr, n3r, gsum, tmp, send, recv, local,
 ):
     a = lax.axis_index("row")
     b = lax.axis_index("col")
@@ -88,7 +88,8 @@
     dev_k = {"col": z * 2 + 1 - k}
     sent = []
 
-    def cp(src, dst, sem, dev):
+    def cp(src, dst, dev):
+        sem = len(sent)
         copy = pltpu.make_async_remote_copy(
             src_ref=src, dst_ref=dst, send_sem=send.at[sem], recv_sem=recv.at[sem],
             device_id=dev, device_id_type=pl.DeviceIdType.MESH,
@@ -117,23 +118,23 @@
         pl.semaphore_signal(barrier, inc=1, device_id=peer, device_id_type=pl.DeviceIdType.MESH)
     pl.semaphore_wait(barrier, len(peers))
 
-    def ring_start(data, ra, rb, me, dev, sem):
+    def ring_start(data, ra, rb, me, dev):
         m1, m2, m3 = (me + 1) % 4, (me + 2) % 4, (me + 3) % 4
         return [
-            cp(data(0, m2), ra(0), sem, dev(1)),
-            cp(data(1, m2), ra(1), sem + 1, dev(3)),
-            cp(data(0, m3), rb(0), sem + 2, dev(3)),
-            cp(data(1, m1), rb(1), sem + 3, dev(1)),
+            cp(data(0, m2), ra(0), dev(1)),
+            cp(data(1, m2), ra(1), dev(3)),
+            cp(data(0, m3), rb(0), dev(3)),
+            cp(data(1, m1), rb(1), dev(1)),
         ]
 
-    def ring_middle(copies, data, ra, rc, me, dev, sem):
+    def ring_middle(copies, data, ra, rc, me, dev):
         m1, m3 = (me + 1) % 4, (me + 3) % 4
         copies[0].wait_recv()
         data(0, m1)[...] += ra(0)[...]
-        c0 = cp(data(0, m1), rc(0), sem + 4, dev(1))
+        c0 = cp(data(0, m1), rc(0), dev(1))
         copies[1].wait_recv()
         data(1, m3)[...] += ra(1)[...]
-        c1 = cp(data(1, m3), rc(1), sem + 5, dev(3))
+        c1 = cp(data(1, m3), rc(1), dev(3))
         return [copies[2], copies[3], c0, c1]
 
     def ring_end(copies, data, rb, rc, me):
@@ -141,6 +142,13 @@
             copy.wait_recv()
         for h in (0, 1):
             data(h, me)[...] += rb(h)[...] + rc(h)[...]
+
+    def to_three(src, dst, dev):
+        return [cp(src(d), dst(d), dev(d)) for d in (1, 2, 3)]
+
+    def wait_all(copies):
+        for copy in copies:
+            copy.wait_recv()
 
     loads[0].wait()
     tokens = []
@@ -187,10 +195,10 @@
 
     loads[1].wait()
     project(gw, gate, False)
-    g1 = ring_start(gate_data, buf(ra1, 0), buf(rb1, 0), x, dev_x, 0)
+    g1 = ring_start(gate_data, buf(ra1, 0), buf(rb1, 0), x, dev_x)
     loads[2].wait()
     project(uw, up, True)
-    u1 = ring_start(up_data, buf(ra1, 1), buf(rb1, 1), y, dev_y, 6)
+    u1 = ring_start(up_data, buf(ra1, 1), buf(rb1, 1), y, dev_y)
 
     def cov_step(step, carry):
         slot = step % 2
@@ -208,15 +216,15 @@
         return carry
 
     lax.fori_loop(0, COV_STEPS // 2, cov_step, 0)
-    g1 = ring_middle(g1, gate_data, buf(ra1, 0), buf(rc1, 0), x, dev_x, 0)
-    u1 = ring_middle(u1, up_data, buf(ra1, 1), buf(rc1, 1), y, dev_y, 6)
+    g1 = ring_middle(g1, gate_data, buf(ra1, 0), buf(rc1, 0), x, dev_x)
+    u1 = ring_middle(u1, up_data, buf(ra1, 1), buf(rc1, 1), y, dev_y)
     lax.fori_loop(COV_STEPS // 2, COV_STEPS, cov_step, 0)
     ring_end(g1, gate_data, buf(rb1, 0), buf(rc1, 0), x)
-    g2 = ring_start(gate_data2, buf(ra2, 0), buf(rb2, 0), y, dev_y, 12)
+    g2 = ring_start(gate_data2, buf(ra2, 0), buf(rb2, 0), y, dev_y)
     ring_end(u1, up_data, buf(rb1, 1), buf(rc1, 1), y)
-    u2 = ring_start(up_data2, buf(ra2, 1), buf(rb2, 1), x, dev_x, 18)
-    g2 = ring_middle(g2, gate_data2, buf(ra2, 0), buf(rc2, 0), y, dev_y, 12)
-    u2 = ring_middle(u2, up_data2, buf(ra2, 1), buf(rc2, 1), x, dev_x, 18)
+    u2 = ring_start(up_data2, buf(ra2, 1), buf(rb2, 1), x, dev_x)
+    g2 = ring_middle(g2, gate_data2, buf(ra2, 0), buf(rc2, 0), y, dev_y)
+    u2 = ring_middle(u2, up_data2, buf(ra2, 1), buf(rc2, 1), x, dev_x)
     ring_end(g2, gate_data2, buf(rb2, 0), buf(rc2, 0), y)
     ring_end(u2, up_data2, buf(rb2, 1), buf(rc2, 1), x)
 
@@ -229,38 +237,31 @@
     piece[0] = 4.0 / math.sqrt(FF) * keys
     top, low = pl.ds(0, 88), pl.ds(88, 80)
 
-    def gather_start(field, own, sem):
+    def gather_start(field, own):
         field[x, y] = piece[own]
-        return [cp(field.at[x, y, top], field.at[x, y, top], sem + d - 1, dev_x(d)) for d in (1, 2, 3)] + [
-            cp(field.at[x, y, low], field.at[x, y, low], sem + 2 + d, dev_y(d)) for d in (1, 2, 3)
-        ]
-
-    def gather_middle(copies, field, sem):
-        for copy in copies[:3]:
+        at, ab = field.at[x, y, top], field.at[x, y, low]
+        return to_three(lambda d: at, lambda d: at, dev_x) + to_three(lambda d: ab, lambda d: ab, dev_y)
+
+    def gather_middle(copies, field):
+        wait_all(copies[:3])
+        mine = field.at[:, y, top]
+        out_y = [cp(mine, mine, dev_y(1)), cp(mine, mine, dev_y(3))]
+        wait_all(copies[3:])
+        mine = field.at[x, :, low]
+        return out_y + [cp(mine, mine, dev_x(1)), cp(mine, mine, dev_x(3))]
+
+    def gather_forward(copies, field):
+        parts = (
+            (field.at[:, (y + 3) % 4, pl.ds(0, 48)], dev_y(1)),
+            (field.at[:, (y + 1) % 4, pl.ds(48, 40)], dev_y(3)),
+            (field.at[(x + 3) % 4, :, pl.ds(88, 40)], dev_x(1)),
+            (field.at[(x + 1) % 4, :, pl.ds(128, 40)], dev_x(3)),
+        )
+        sends = []
+        for copy, (block, dev) in zip(copies, parts):
             copy.wait_recv()
-        mine = field.at[:, y, top]
-        out_y = [cp(mine, mine, sem + 6, dev_y(1)), cp(mine, mine, sem + 7, dev_y(3))]
-        for copy in copies[3:]:
-            copy.wait_recv()
-        mine = field.at[x, :, low]
-        out_x = [cp(mine, mine, sem + 8, dev_x(1)), cp(mine, mine, sem + 9, dev_x(3))]
-        return out_y + out_x
-
-    def gather_forward(copies, field, sem):
-        y1, y3, x1, x3 = (y + 1) % 4, (y + 3) % 4, (x + 1) % 4, (x + 3) % 4
-        copies[0].wait_recv()
-        part0 = field.at[:, y3, pl.ds(0, 48)]
-        f0 = cp(part0, part0, sem + 10, dev_y(1))
-        copies[1].wait_recv()
-        part1 = field.at[:, y1, pl.ds(48, 40)]
-        f1 = cp(part1, part1, sem + 11, dev_y(3))
-        copies[2].wait_recv()
-        part2 = field.at[x3, :, pl.ds(88, 40)]
-        f2 = cp(part2, part2, sem + 12, dev_x(1))
-        copies[3].wait_recv()
-        part3 = field.at[x1, :, pl.ds(128, 40)]
-        f3 = cp(part3, part3, sem + 13, dev_x(3))
-        return [f0, f1, f2, f3]
+            sends.append(cp(block, block, dev))
+        return sends
 
     def split_field(field, target):
         def body(i, carry):
@@ -285,19 +286,22 @@
         both = dot_b(chi[rows, :], target[...])
         return both[:, :E] + (both[:, E:] + dot_b(clo[rows, :], target[:, :E]))
 
-    bg = gather_start(bc, 0, 24)
+    bg = gather_start(bc, 0)
 
     loads[3].wait()
     tp[...] = jnp.zeros_like(tp)
     tp[0:42, :] = tgt[...]
     first = (a * 8 + b) * 42
+    t_high, t_rest = tp[...].astype(BF16), tp[...] - tp[...].astype(BF16).astype(F32)
+    t_mid, t_low = halves(t_rest)
+    t_all = jnp.concatenate([t_high, t_mid, t_low], axis=0)
+    minus = -keys_half
 
     def current(j, carry):
         at = pl.multiple_of(j * 384, 128)
-        value = dot_tb(keys_half, dw[:, pl.ds(at, 384)])
         place = lax.broadcasted_iota(jnp.int32, (48, 384), 1) + j * 384 - first
-        mark = jnp.where(place == lax.broadcasted_iota(jnp.int32, (48, 384), 0), 1.0, 0.0)
-        value = dot_t(tp[...], mark) - value
+        mark = jnp.where(place == lax.broadcasted_iota(jnp.int32, (48, 384), 0), 1.0, 0.0).astype(BF16)
+        value = dot_tb(minus, dw[:, pl.ds(at, 384)]) + dot_tb(t_all, jnp.concatenate([mark, mark, mark], axis=0))
         for i in range(3):
             part[j * 3 + i] = value[:, i * E : (i + 1) * E]
         return carry
@@ -310,12 +314,17 @@
     def half_of(kk):
         return pl.ds(pl.multiple_of(kk * 64, 8), 64)
 
-    p1 = cp(part.at[real, half_of(1 - k)], rk, 52, dev_k)
-    bg = gather_middle(bg, bc, 24)
+    def rows_of(zz, h):
+        return pl.ds(pl.multiple_of(k * 64 + zz * 16 + h * 8, 8), 8)
 
     def part_data(h, t):
-        return part.at[real, pl.ds(pl.multiple_of(k * 64 + t * 16 + h * 8, 8), 8)]
-
+        return part.at[real, rows_of(t, h)]
+
+    def at_half(ref):
+        return lambda h: ref.at[h]
+
+    p1 = cp(part.at[real, half_of(1 - k)], rk, dev_k)
+    bg = gather_middle(bg, bc)
     p1.wait_recv()
 
     def add_half(i, carry):
@@ -323,13 +332,31 @@
         return carry
 
     lax.fori_loop(0, 42, add_half, 0)
-    bf = gather_forward(bg, bc, 24)
-    pz = ring_start(part_data, lambda h: pa.at[h], lambda h: pb.at[h], z, dev_z, 53)
-    for copy in bf:
+    pz = ring_start(part_data, at_half(pa), at_half(pb), z, dev_z)
+    bf = gather_forward(bg, bc)
+    wait_all(bf)
+    split_field(bc, bhl)
+
+    def halve(ref, i, value):
+        ref[i, 0] = value[:64]
+        ref[i, 1] = value[64:]
+
+    def cores_start(ref, n, got):
+        return cp(ref.at[pl.ds(0, n), 1 - k], got.at[pl.ds(0, n)], dev_k)
+
+    def cores_end(copy, ref, n, got):
         copy.wait_recv()
-    split_field(bc, bhl)
-    m0[0] = gram(bhl, bhl)
-    mk = cp(m0.at[0], m0.at[1], 59, dev_k)
+        ref[pl.ds(0, n), k] += got[pl.ds(0, n)]
+
+    def axis_start(ref, n, got, dev):
+        return to_three(lambda d: ref.at[pl.ds(0, n), k], lambda d: got.at[d - 1, pl.ds(0, n)], dev)
+
+    def axis_end(copies, ref, n, got, target):
+        wait_all(copies)
+        target[pl.ds(0, n), k] = ref[pl.ds(0, n), k] + ((got[0, pl.ds(0, n)] + got[1, pl.ds(0, n)]) + got[2, pl.ds(0, n)])
+
+    def cores_share(ref):
+        return cp(ref.at[:, k], ref.at[:, k], dev_k)
 
     def first_image(i, carry):
         value = cov_times(i, bhl)
@@ -338,8 +365,9 @@
         return carry
 
     lax.fori_loop(0, 4, first_image, 0)
-    v1 = cp(vv.at[:, 1 - k], vk, 60, dev_k)
-    pz = ring_middle(pz, part_data, lambda h: pa.at[h], lambda h: pc.at[h], z, dev_z, 53)
+    v1 = cp(vv.at[:, 1 - k], vk, dev_k)
+    halve(m0, 0, gram(bhl, bhl))
+    mk = cores_start(m0, 1, mc)
     v1.wait_recv()
     vv[:, k] += vk[...]
 
@@ -349,104 +377,96 @@
     def image_buf(ref):
         return lambda h: ref.at[h, pl.ds(0, 88 if h == 0 else 80)]
 
-    vz = ring_start(image_data, image_buf(va), image_buf(vb), z, dev_z, 61)
-    mk.wait_recv()
-    m0[2] = m0[0] + m0[1]
-    vz = ring_middle(vz, image_data, image_buf(va), image_buf(vc), z, dev_z, 61)
-    mz = [cp(m0.at[2], m0.at[2 + d], 66 + d, dev_z(d)) for d in (1, 2, 3)]
+    vz = ring_start(image_data, image_buf(va), image_buf(vb), z, dev_z)
+    pz = ring_middle(pz, part_data, at_half(pa), at_half(pc), z, dev_z)
+    vz = ring_middle(vz, image_data, image_buf(va), image_buf(vc), z, dev_z)
+    cores_end(mk, m0, 1, mc)
     ring_end(vz, image_data, image_buf(vb), image_buf(vc), z)
     piece[1] = vv[z, k]
-    wg = gather_start(wc, 1, 38)
+    wg = gather_start(wc, 1)
     wr[z, k] = piece[1]
-    wz = [cp(wr.at[z, k], wr.at[z, k], 69 + d, dev_z(d)) for d in (1, 2, 3)]
-    ring_end(pz, part_data, lambda h: pb.at[h], lambda h: pc.at[h], z)
-    wg = gather_middle(wg, wc, 38)
-    wf = gather_forward(wg, wc, 38)
-    own_rows = pl.ds(pl.multiple_of(k * 64 + z * 16, 8), 16)
+    wz = to_three(lambda d: wr.at[z, k], lambda d: wr.at[z, k], dev_z)
+    mz = axis_start(m0, 1, mzr, dev_z)
+    ring_end(pz, part_data, at_half(pb), at_half(pc), z)
 
     def twelve(t):
         return pl.ds(t * 12, 12)
 
-    px = [cp(part.at[twelve((x + d) % 4), own_rows], xr.at[d - 1], 72 + d, dev_x(d)) for d in (1, 2, 3)]
-    for copy in wz:
-        copy.wait_recv()
-    wk = cp(wr.at[:, k], wr.at[:, k], 76, dev_k)
-    for copy in mz:
-        copy.wait_recv()
-    gram0 = sym((m0[2] + m0[3]) + (m0[4] + m0[5]))
-    for copy in wf:
-        copy.wait_recv()
+    def three(t, u):
+        return pl.ds(t * 12 + u * 3, 3)
+
+    up_rows, down_rows = rows_of(z, 0), rows_of(z, 1)
+    wg = gather_middle(wg, wc)
+    px = to_three(lambda d: part.at[twelve((x + d) % 4), up_rows], lambda d: xr.at[0, d - 1], dev_x)
+    px += to_three(lambda d: part.at[twelve((y + d) % 4), down_rows], lambda d: xr.at[1, d - 1], dev_y)
+    wait_all(wz)
+    wk = cp(wr.at[:, k], wr.at[:, k], dev_k)
+    axis_end(mz, m0, 1, mzr, gsum)
+    wf = gather_forward(wg, wc)
+    wait_all(px)
+    part[twelve(x), up_rows] += (xr[0, 0] + xr[0, 1]) + xr[0, 2]
+    part[twelve(y), down_rows] += (xr[1, 0] + xr[1, 1]) + xr[1, 2]
+    py = to_three(lambda d: part.at[three(x, (y + d) % 4), up_rows], lambda d: yr.at[0, d - 1], dev_y)
+    py += to_three(lambda d: part.at[three(y, (x + d) % 4), down_rows], lambda d: yr.at[1, d - 1], dev_x)
+    wait_all(wf)
     split_field(wc, whl)
-    n12[0, 0] = gram(bhl, whl)
-    n12[0, 1] = gram(whl, whl)
-    nk = cp(n12.at[0], n12.at[1], 77, dev_k)
+    halve(n12, 0, gram(bhl, whl))
+    halve(n12, 1, gram(whl, whl))
+    nk = cores_start(n12, 2, nc)
+    wait_all(py)
+    res[three(x, y), up_rows] = part[three(x, y), up_rows] + ((yr[0, 0] + yr[0, 1]) + yr[0, 2])
+    res[three(y, x), down_rows] = part[three(y, x), down_rows] + ((yr[1, 0] + yr[1, 1]) + yr[1, 2])
+    own_a, own_b = res.at[three(x, y), up_rows], res.at[three(y, x), down_rows]
+    ry = to_three(lambda d: own_a, lambda d: own_a, dev_y) + to_three(lambda d: own_b, lambda d: own_b, dev_x)
     wk.wait_recv()
 
     def second_image(i, total):
         value = cov_times(i, whl)
         return total + dot_t(wr[i].reshape(336, E), value)
 
-    n3[0] = lax.fori_loop(0, 4, second_image, jnp.zeros((E, E), F32))
-    n3k = cp(n3.at[0], n3.at[1], 78, dev_k)
-    nk.wait_recv()
-    n12[2] = n12[0] + n12[1]
-    nz = [cp(n12.at[2], n12.at[2 + d], 78 + d, dev_z(d)) for d in (1, 2, 3)]
-    n3k.wait_recv()
-    n3[2] = n3[0] + n3[1]
-    n3z = [cp(n3.at[2], n3.at[2 + d], 81 + d, dev_z(d)) for d in (1, 2, 3)]
-
-    for copy in px:
-        copy.wait_recv()
-    part[twelve(x), own_rows] += (xr[0] + xr[1]) + xr[2]
-
-    def three(t):
-        return pl.ds(x * 12 + t * 3, 3)
-
-    py = [cp(part.at[three((y + d) % 4), own_rows], yr.at[d - 1], 84 + d, dev_y(d)) for d in (1, 2, 3)]
-    for copy in nz:
-        copy.wait_recv()
-    both = (n12[2] + n12[3]) + (n12[4] + n12[5])
-    n1, n2 = sym(both[0]), both[1]
+    total = lax.fori_loop(0, 2, second_image, jnp.zeros((E, E), F32))
+    cores_end(nk, n12, 2, nc)
+    nz = axis_start(n12, 2, nzr, dev_z)
+    wait_all(ry)
+    own_a, own_b = res.at[twelve(x), up_rows], res.at[twelve(y), down_rows]
+    rx = to_three(lambda d: own_a, lambda d: own_a, dev_x) + to_three(lambda d: own_b, lambda d: own_b, dev_y)
+    total = lax.fori_loop(2, 4, second_image, total)
+    halve(n3, 0, total)
+    n3k = cores_start(n3, 1, mc2)
+    axis_end(nz, n12, 2, nzr, gsum.at[pl.ds(1, 2)])
+    gs = cores_share(gsum)
+    wait_all(rx)
+    own_z = res.at[real, pl.ds(pl.multiple_of(k * 64 + z * 16, 8), 16)]
+    rz = [cp(own_z, own_z, dev_z(1)), cp(own_z, own_z, dev_z(3))]
+    cores_end(n3k, n3, 1, mc2)
+    n3y = axis_start(n3, 1, n3r.at[0], dev_y)
+    gs.wait_recv()
+
+    def whole(ref, i):
+        return jnp.concatenate([ref[i, 0], ref[i, 1]], axis=0)
+
+    gram0, n1, n2 = sym(whole(gsum, 0)), sym(whole(gsum, 1)), sym(whole(gsum, 2))
     square = dot(gram0, gram0)
     m1 = sym(n1 + square)
+    axis_end(n3y, n3, 1, n3r.at[0], n3.at[pl.ds(1, 1)])
+    n3x = axis_start(n3.at[pl.ds(1, 1)], 1, n3r.at[1], dev_x)
+    inv0, inv1 = sweep_some(5, gram0, m1)
+    axis_end(n3x, n3.at[pl.ds(1, 1)], 1, n3r.at[1], n3.at[pl.ds(2, 1)])
+    n3z = axis_start(n3.at[pl.ds(2, 1)], 1, n3r.at[2], dev_z)
+    inv0, inv1 = sweep_some(6, inv0, inv1)
+    rz[0].wait_recv()
+    fwd0 = res.at[real, rows_of((z + 3) % 4, 0)]
+    rf0 = cp(fwd0, fwd0, dev_z(1))
+    rz[1].wait_recv()
+    fwd1 = res.at[real, rows_of((z + 1) % 4, 1)]
+    rf1 = cp(fwd1, fwd1, dev_z(3))
+    axis_end(n3z, n3.at[pl.ds(2, 1)], 1, n3r.at[2], n3.at[pl.ds(3, 1)])
+    n3s = cores_share(n3.at[pl.ds(3, 1)])
+    inv0, inv1 = sweep_some(5, inv0, inv1)
     n1m0 = dot(n1, gram0)
     m2 = sym(n2 + n1m0 + n1m0.T + dot(square, gram0))
     n2m0 = dot(n2, gram0)
     m3_rest = sym(n2m0 + n2m0.T + dot(gram0, n1m0) + dot(m1, m1))
-    for copy in n3z:
-        copy.wait_recv()
-    n3[6] = (n3[2] + n3[3]) + (n3[4] + n3[5])
-    n3y = [cp(n3.at[6], n3.at[6 + d], 87 + d, dev_y(d)) for d in (1, 2, 3)]
-    for copy in py:
-        copy.wait_recv()
-    res[three(y), own_rows] = part[three(y), own_rows] + ((yr[0] + yr[1]) + yr[2])
-    mine = res.at[three(y), own_rows]
-    ry = [cp(mine, mine, 90 + d, dev_y(d)) for d in (1, 2, 3)]
-    inv0, inv1 = sweep_some(4, gram0, m1)
-    for copy in n3y:
-        copy.wait_recv()
-    n3[10] = (n3[6] + n3[7]) + (n3[8] + n3[9])
-    n3x = [cp(n3.at[10], n3.at[10 + d], 93 + d, dev_x(d)) for d in (1, 2, 3)]
-    for copy in ry:
-        copy.wait_recv()
-    mine_x = res.at[twelve(x), own_rows]
-    rx = [cp(mine_x, mine_x, 96 + d, dev_x(d)) for d in (1, 2, 3)]
-    inv0, inv1 = sweep_some(6, inv0, inv1)
-    for copy in rx:
-        copy.wait_recv()
-    mine_z = res.at[real, own_rows]
-    rz = [cp(mine_z, mine_z, 100, dev_z(1)), cp(mine_z, mine_z, 101, dev_z(3))]
-    inv0, inv1 = sweep_some(6, inv0, inv1)
-
-    def rows_of(zz, h):
-        return pl.ds(pl.multiple_of(k * 64 + zz * 16 + h * 8, 8), 8)
-
-    rz[0].wait_recv()
-    fwd0 = res.at[real, rows_of((z + 3) % 4, 0)]
-    rf0 = cp(fwd0, fwd0, 102, dev_z(1))
-    rz[1].wait_recv()
-    fwd1 = res.at[real, rows_of((z + 1) % 4, 1)]
-    rf1 = cp(fwd1, fwd1, 103, dev_z(3))
     alpha0 = dot(inv1, gram0)
     norm1 = sym(dot_t(alpha0, dot(m2, alpha0)) - gram0)
     beta = dot(inv0, norm1)
@@ -456,20 +476,18 @@
     c1 = eye + beta
     cross = dot_t(c1, dot(m2, alpha0))
     curv_rest = dot_t(c1, dot(m1, c1)) - cross - cross.T
-    for copy in n3x:
-        copy.wait_recv()
-    m3 = m3_rest + sym((n3[10] + n3[11]) + (n3[12] + n3[13]))
+    n3s.wait_recv()
+    m3 = m3_rest + sym(whole(n3, 3))
     curvature = sym(curv_rest + dot_t(alpha0, dot(m3, alpha0)))
+    wait_all([rf0, rf1])
+    half = res.at[real, half_of(k)]
+    rkk = cp(half, half, dev_k)
     (inv2,) = sweep_some(16, curvature)
-    rf0.wait_recv()
-    rf1.wait_recv()
-    half = res.at[real, half_of(k)]
-    rkk = cp(half, half, 104, dev_k)
     alpha1 = dot(inv2, norm1)
     on_w = -dot(alpha0, alpha1)
-    m0[3] = dot(c1, alpha1)
-    m0[4] = dot(gram0, on_w)
-    on_b = alpha0 + (m0[3] + m0[4])
+    tmp[0] = dot(c1, alpha1)
+    tmp[1] = dot(gram0, on_w)
+    on_b = alpha0 + (tmp[0] + tmp[1])
     fh, fl = halves(jnp.concatenate([piece[0], piece[1]], axis=1))
     ch, cl = halves(jnp.concatenate([on_b, on_w], axis=0))
     found = dot_b(fh, ch) + (dot_b(fh, cl) + dot_b(fl, ch))
@@ -531,13 +549,21 @@
             small(2, 42, 8, E),
             small(2, 42, 8, E),
             small(2, 42, 8, E),
-            small(3, 12, 16, E),
-            small(3, 3, 16, E),
+            small(2, 3, 12, 8, E),
+            small(2, 3, 3, 8, E),
             small(48, E, E),
             small(48, E),
-            small(6, E, E),
-            small(6, 2, E, E),
-            small(14, E, E),
+            small(1, 2, 64, E),
+            small(2, 2, 64, E),
+            small(4, 2, 64, E),
+            small(1, 64, E),
+            small(2, 64, E),
+            small(1, 64, E),
+            small(3, 1, 64, E),
+            small(3, 2, 64, E),
+            small(3, 3, 1, 64, E),
+            small(3, 2, 64, E),
+            small(2, E, E),
             pltpu.SemaphoreType.DMA((N_SEM,)),
             pltpu.SemaphoreType.DMA((N_SEM,)),
             pltpu.SemaphoreType.DMA((6,)),

time: 165 us -> 149 us (0.903)
  Pallas kernels: 161 us -> 146 us
    pallas_call x1, Pallas kernels: 161 us -> 146 us  [body(): pl.pallas_call(kernel, out_shape=jax.ShapeDtypeStruct((PIECE, D), BF16),...]
where the time goes in v2:
time: 149 us
  Pallas kernels  146 us (98%)
  local copies, waits for them, and re-layouts  2.83 us (2%)
    pallas_call x1, Pallas kernels, body(): pl.pallas_call(kernel, out_shape=jax.ShapeDtypeStruct((PIECE, D), BF16),...  146 us

profile of v2, /device:TPU:1, one launch (start us, length us, event | category | flops | bytes accessed | tf_op | source)
XLA Modules:
  0.0 148.6 jit_solution(5559329944343320406)
XLA Ops:
  0.0 145.7 %edit.1 = bf16[168,5376]{1,0:T(8,128)(2,1)} custom-call(bf16[2,8,336,128]{3,2,1,0:T(8,128)(2,1)} %bitcast.12, s32[2,128]{1,0:T(2,128)} %bitcast.13, bf16[336,2688]{1,0:T(8,128)(2,1)} %bitcast.9, bf16[336,2688]{1,0:T(8,128)(2,1)} %bitcast.10, bf16[168,5376]{1,0:T(8,128)(2,1)} %bitcast.11, f32[28224,128]{1,0:T(8,128)} %bitcast.7, f32[42,128]{1,0:T(8,128)} %tgt.1), custom_call_target="tpu_custom_call" | custom-call | tf_op jit(solution)/shard_map/edit/pallas_call | solution.py:514
  145.7 2.8 %copy.9 = bf16[1,1,168,5376]{3,2,1,0:T(8,128)(2,1)} copy(bf16[1,1,168,5376]{3,2,1,0:T(8,128)(2,1)} %bitcast.8) | data formatting | bytes 3612672

commit v3 on v2

--- a/solution.py
+++ b/solution.py
@@ -14,7 +14,7 @@
 F32 = jnp.float32
 BF16 = jnp.bfloat16
 HI = lax.Precision.HIGHEST
-N_SEM = 132
+N_SEM = 180
 COV_ROWS = 112
 COV_STEPS = 1344 // COV_ROWS
 LINES = COV_ROWS * 21
@@ -67,9 +67,9 @@
 def kernel(
     states_h, pos, gw_h, uw_h, dw_h, cov_h, tgt,
     out,
-    states, gw, uw, dw, cbuf, flat, gate, up, ra1, rb1, rc1, ra2, rb2, rc2,
-    chi, clo, piece, bc, wc, bhl, whl, vv, vk, va, vb, vc, wr,
-    part, rk, pa, pb, pc, xr, yr, res, tp, m0, n12, n3, mc, nc, mc2, mzr, nzr, n3r, gsum, tmp, send, recv, local,
+    states, gw, uw, dw, cbuf, gate, up, ra1, rb1, rc1, ra2,
+    chi, clo, piece, bc, wc, bhl, whl, vv, vk, va, wr,
+    part, rk, pa, xr, res, tp, m0, n12, n3, mc, nc, mc2, mzr, nzr, n3r, gsum, tmp, send, recv, local,
 ):
     a = lax.axis_index("row")
     b = lax.axis_index("col")
@@ -84,6 +84,11 @@
 
     def dev_z(d):
         return {"col": ((z + d) % 4) * 2 + k}
+
+    others = [(i, j) for i in range(4) for j in range(4) if i + j > 0]
+
+    def dev_xy(i, j):
+        return {"row": ((x + i) % 4) * 4 + (y + j) % 4}
 
     dev_k = {"col": z * 2 + 1 - k}
     sent = []
@@ -113,19 +118,18 @@
     cov_load(0, 0).start()
 
     barrier = pltpu.get_barrier_semaphore()
-    peers = [dev(d) for dev in (dev_x, dev_y, dev_z) for d in (1, 2, 3)] + [dev_k]
+    peers = [dev_z(d) for d in (1, 2, 3)] + [dev_k]
+    peers += [dev_xy(i, j) for i, j in others]
     for peer in peers:
         pl.semaphore_signal(barrier, inc=1, device_id=peer, device_id_type=pl.DeviceIdType.MESH)
     pl.semaphore_wait(barrier, len(peers))
 
-    def ring_start(data, ra, rb, me, dev):
-        m1, m2, m3 = (me + 1) % 4, (me + 2) % 4, (me + 3) % 4
-        return [
-            cp(data(0, m2), ra(0), dev(1)),
-            cp(data(1, m2), ra(1), dev(3)),
-            cp(data(0, m3), rb(0), dev(3)),
-            cp(data(1, m1), rb(1), dev(1)),
-        ]
+    def ring_far(data, ra, me, dev):
+        m2 = (me + 2) % 4
+        return [cp(data(0, m2), ra(0), dev(1)), cp(data(1, m2), ra(1), dev(3))]
+
+    def ring_near(data, rb, me, dev):
+        return [cp(data(0, (me + 3) % 4), rb(0), dev(3)), cp(data(1, (me + 1) % 4), rb(1), dev(1))]
 
     def ring_middle(copies, data, ra, rc, me, dev):
         m1, m3 = (me + 1) % 4, (me + 3) % 4
@@ -135,7 +139,7 @@
         copies[1].wait_recv()
         data(1, m3)[...] += ra(1)[...]
         c1 = cp(data(1, m3), rc(1), dev(3))
-        return [copies[2], copies[3], c0, c1]
+        return [c0, c1]
 
     def ring_end(copies, data, rb, rc, me):
         for copy in copies:
@@ -161,22 +165,17 @@
     tokens = jnp.concatenate(tokens, axis=1)
 
     def project(weight, target, by_y):
-        def chunk(j, carry):
-            at = pl.multiple_of(j * 384, 128)
-            flat[pl.ds(at, 384), :] = dot_tb(weight[:, pl.ds(at, 384)], tokens)
-            return carry
-
-        lax.fori_loop(0, 7, chunk, 0)
-
-        def place(i, carry):
-            px, py = i // 4, i % 4
-            first, second = (py, px) if by_y else (px, py)
-            at = pl.multiple_of(i * PIECE, 8)
-            for p in (0, 1):
-                target[p, first, second] = flat[pl.ds(at, PIECE), p * E : (p + 1) * E]
-            return carry
-
-        lax.fori_loop(0, 16, place, 0)
+        for j in range(7):
+            value = dot_tb(weight[:, j * 384 : (j + 1) * 384], tokens)
+            row = j * 384
+            while row < (j + 1) * 384:
+                block, off = row // PIECE, row % PIECE
+                size = min(PIECE - off, (j + 1) * 384 - row)
+                first, second = (block % 4, block // 4) if by_y else (block // 4, block % 4)
+                lines = value[row - j * 384 : row - j * 384 + size]
+                target[0, first, second, off : off + size] = lines[:, :E]
+                target[1, first, second, off : off + size] = lines[:, E:]
+                row += size
 
     def gate_data(h, t):
         return gate.at[h, t]
@@ -184,21 +183,8 @@
     def up_data(h, t):
         return up.at[h, t]
 
-    def gate_data2(h, t):
-        return gate.at[h, x, t]
-
-    def up_data2(h, t):
-        return up.at[h, y, t]
-
     def buf(ref, which):
         return lambda h: ref.at[which, h]
-
-    loads[1].wait()
-    project(gw, gate, False)
-    g1 = ring_start(gate_data, buf(ra1, 0), buf(rb1, 0), x, dev_x)
-    loads[2].wait()
-    project(uw, up, True)
-    u1 = ring_start(up_data, buf(ra1, 1), buf(rb1, 1), y, dev_y)
 
     def cov_step(step, carry):
         slot = step % 2
@@ -215,23 +201,32 @@
             clo[rows, t * E : (t + 1) * E] = low
         return carry
 
-    lax.fori_loop(0, COV_STEPS // 2, cov_step, 0)
-    g1 = ring_middle(g1, gate_data, buf(ra1, 0), buf(rc1, 0), x, dev_x)
-    u1 = ring_middle(u1, up_data, buf(ra1, 1), buf(rc1, 1), y, dev_y)
-    lax.fori_loop(COV_STEPS // 2, COV_STEPS, cov_step, 0)
-    ring_end(g1, gate_data, buf(rb1, 0), buf(rc1, 0), x)
-    g2 = ring_start(gate_data2, buf(ra2, 0), buf(rb2, 0), y, dev_y)
-    ring_end(u1, up_data, buf(rb1, 1), buf(rc1, 1), y)
-    u2 = ring_start(up_data2, buf(ra2, 1), buf(rb2, 1), x, dev_x)
-    g2 = ring_middle(g2, gate_data2, buf(ra2, 0), buf(rc2, 0), y, dev_y)
-    u2 = ring_middle(u2, up_data2, buf(ra2, 1), buf(rc2, 1), x, dev_x)
-    ring_end(g2, gate_data2, buf(rb2, 0), buf(rc2, 0), y)
-    ring_end(u2, up_data2, buf(rb2, 1), buf(rc2, 1), x)
+    loads[1].wait()
+    project(gw, gate, False)
+    g_far = ring_far(gate_data, buf(ra1, 0), x, dev_x)
+    loads[2].wait()
+    project(uw, up, True)
+    u_far = ring_far(up_data, buf(ra1, 1), y, dev_y)
+    g_near = ring_near(gate_data, buf(rb1, 0), x, dev_x)
+    lax.fori_loop(0, 3, cov_step, 0)
+    u_near = ring_near(up_data, buf(rb1, 1), y, dev_y)
+    lax.fori_loop(3, 6, cov_step, 0)
+    g_near += ring_middle(g_far, gate_data, buf(ra1, 0), buf(rc1, 0), x, dev_x)
+    lax.fori_loop(6, 8, cov_step, 0)
+    u_near += ring_middle(u_far, up_data, buf(ra1, 1), buf(rc1, 1), y, dev_y)
+    lax.fori_loop(8, COV_STEPS, cov_step, 0)
+    ring_end(g_near, gate_data, buf(rb1, 0), buf(rc1, 0), x)
+    g2 = to_three(lambda d: gate.at[:, x, (y + d) % 4], lambda d: ra2.at[0, d - 1], dev_y)
+    ring_end(u_near, up_data, buf(rb1, 1), buf(rc1, 1), y)
+    u2 = to_three(lambda d: up.at[:, y, (x + d) % 4], lambda d: ra2.at[1, d - 1], dev_x)
+    wait_all(g2)
+    wait_all(u2)
 
     keys = jnp.zeros((PIECE, E), F32)
     for p in (0, 1):
-        v = gate[p, x, y]
-        keys = keys + v / (1.0 + jnp.exp(-v)) * up[p, y, x]
+        v = gate[p, x, y] + ((ra2[0, 0, p] + ra2[0, 1, p]) + ra2[0, 2, p])
+        u = up[p, y, x] + ((ra2[1, 0, p] + ra2[1, 1, p]) + ra2[1, 2, p])
+        keys = keys + v / (1.0 + jnp.exp(-v)) * u
     keys = keys * 0.5
     keys_half = keys.astype(BF16)
     piece[0] = 4.0 / math.sqrt(FF) * keys
@@ -240,28 +235,20 @@
     def gather_start(field, own):
         field[x, y] = piece[own]
         at, ab = field.at[x, y, top], field.at[x, y, low]
-        return to_three(lambda d: at, lambda d: at, dev_x) + to_three(lambda d: ab, lambda d: ab, dev_y)
-
-    def gather_middle(copies, field):
-        wait_all(copies[:3])
-        mine = field.at[:, y, top]
-        out_y = [cp(mine, mine, dev_y(1)), cp(mine, mine, dev_y(3))]
-        wait_all(copies[3:])
-        mine = field.at[x, :, low]
-        return out_y + [cp(mine, mine, dev_x(1)), cp(mine, mine, dev_x(3))]
-
-    def gather_forward(copies, field):
-        parts = (
-            (field.at[:, (y + 3) % 4, pl.ds(0, 48)], dev_y(1)),
-            (field.at[:, (y + 1) % 4, pl.ds(48, 40)], dev_y(3)),
-            (field.at[(x + 3) % 4, :, pl.ds(88, 40)], dev_x(1)),
-            (field.at[(x + 1) % 4, :, pl.ds(128, 40)], dev_x(3)),
-        )
-        sends = []
-        for copy, (block, dev) in zip(copies, parts):
-            copy.wait_recv()
-            sends.append(cp(block, block, dev))
-        return sends
+        first = [cp(at, at, dev_x(d)) for d in (1, 3, 2)] + [cp(ab, ab, dev_y(d)) for d in (1, 3, 2)]
+        return first, [cp(ab, ab, dev_x(d)) for d in (1, 3, 2)] + [cp(at, at, dev_y(d)) for d in (1, 3, 2)]
+
+    def gather_next(copies, field):
+        first, rest = copies
+        rest = list(rest)
+        for i, d in enumerate((3, 1, 2)):
+            first[i].wait_recv()
+            at = field.at[(x + d) % 4, y, top]
+            rest += to_three(lambda e: at, lambda e: at, dev_y)
+            first[i + 3].wait_recv()
+            ab = field.at[x, (y + d) % 4, low]
+            rest += to_three(lambda e: ab, lambda e: ab, dev_x)
+        return rest
 
     def split_field(field, target):
         def body(i, carry):
@@ -314,17 +301,11 @@
     def half_of(kk):
         return pl.ds(pl.multiple_of(kk * 64, 8), 64)
 
-    def rows_of(zz, h):
-        return pl.ds(pl.multiple_of(k * 64 + zz * 16 + h * 8, 8), 8)
-
-    def part_data(h, t):
-        return part.at[real, rows_of(t, h)]
-
-    def at_half(ref):
-        return lambda h: ref.at[h]
+    def rows_of(zz):
+        return pl.ds(pl.multiple_of(k * 64 + zz * 16, 8), 16)
 
     p1 = cp(part.at[real, half_of(1 - k)], rk, dev_k)
-    bg = gather_middle(bg, bc)
+    bg = gather_next(bg, bc)
     p1.wait_recv()
 
     def add_half(i, carry):
@@ -332,9 +313,9 @@
         return carry
 
     lax.fori_loop(0, 42, add_half, 0)
-    pz = ring_start(part_data, at_half(pa), at_half(pb), z, dev_z)
-    bf = gather_forward(bg, bc)
-    wait_all(bf)
+    own_rows = rows_of(z)
+    pz = to_three(lambda d: part.at[real, rows_of((z + d) % 4)], lambda d: pa.at[d - 1], dev_z)
+    wait_all(bg)
     split_field(bc, bhl)
 
     def halve(ref, i, value):
@@ -371,75 +352,62 @@
     v1.wait_recv()
     vv[:, k] += vk[...]
 
-    def image_data(h, t):
-        return vv.at[t, k, top if h == 0 else low]
-
-    def image_buf(ref):
-        return lambda h: ref.at[h, pl.ds(0, 88 if h == 0 else 80)]
-
-    vz = ring_start(image_data, image_buf(va), image_buf(vb), z, dev_z)
-    pz = ring_middle(pz, part_data, at_half(pa), at_half(pc), z, dev_z)
-    vz = ring_middle(vz, image_data, image_buf(va), image_buf(vc), z, dev_z)
+    vz = to_three(lambda d: vv.at[(z + d) % 4, k], lambda d: va.at[d - 1], dev_z)
     cores_end(mk, m0, 1, mc)
-    ring_end(vz, image_data, image_buf(vb), image_buf(vc), z)
-    piece[1] = vv[z, k]
+    wait_all(vz)
+    piece[1] = vv[z, k] + ((va[0] + va[1]) + va[2])
     wg = gather_start(wc, 1)
     wr[z, k] = piece[1]
     wz = to_three(lambda d: wr.at[z, k], lambda d: wr.at[z, k], dev_z)
     mz = axis_start(m0, 1, mzr, dev_z)
-    ring_end(pz, part_data, at_half(pb), at_half(pc), z)
-
-    def twelve(t):
-        return pl.ds(t * 12, 12)
-
-    def three(t, u):
-        return pl.ds(t * 12 + u * 3, 3)
-
-    up_rows, down_rows = rows_of(z, 0), rows_of(z, 1)
-    wg = gather_middle(wg, wc)
-    px = to_three(lambda d: part.at[twelve((x + d) % 4), up_rows], lambda d: xr.at[0, d - 1], dev_x)
-    px += to_three(lambda d: part.at[twelve((y + d) % 4), down_rows], lambda d: xr.at[1, d - 1], dev_y)
+    wg = gather_next(wg, wc)
+
+    def three(xx, yy):
+        return pl.ds(xx * 12 + yy * 3, 3)
+
+    wait_all(pz)
+    part[real, own_rows] += (pa[0] + pa[1]) + pa[2]
+    px = [
+        cp(part.at[three((x + i) % 4, (y + j) % 4), own_rows], xr.at[n], dev_xy(i, j))
+        for n, (i, j) in enumerate(others)
+    ]
     wait_all(wz)
     wk = cp(wr.at[:, k], wr.at[:, k], dev_k)
     axis_end(mz, m0, 1, mzr, gsum)
-    wf = gather_forward(wg, wc)
+    wait_all(wg)
+    split_field(wc, whl)
+    wk.wait_recv()
+
+    def second_image(i, total):
+        value = cov_times(i, whl)
+        return total + dot_t(wr[i].reshape(336, E), value)
+
+    total = lax.fori_loop(0, 4, second_image, jnp.zeros((E, E), F32))
+    halve(n3, 0, total)
+    n3k = cores_start(n3, 1, mc2)
     wait_all(px)
-    part[twelve(x), up_rows] += (xr[0, 0] + xr[0, 1]) + xr[0, 2]
-    part[twelve(y), down_rows] += (xr[1, 0] + xr[1, 1]) + xr[1, 2]
-    py = to_three(lambda d: part.at[three(x, (y + d) % 4), up_rows], lambda d: yr.at[0, d - 1], dev_y)
-    py += to_three(lambda d: part.at[three(y, (x + d) % 4), down_rows], lambda d: yr.at[1, d - 1], dev_x)
-    wait_all(wf)
-    split_field(wc, whl)
+    mine = part[three(x, y), own_rows]
+    for n in range(15):
+        mine = mine + xr[n]
+    res[three(x, y), own_rows] = mine
+    own = res.at[three(x, y), own_rows]
+    rx = [cp(own, own, dev_xy(i, j)) for i, j in others]
+    cores_end(n3k, n3, 1, mc2)
+    n3z = axis_start(n3, 1, n3r.at[0], dev_z)
     halve(n12, 0, gram(bhl, whl))
     halve(n12, 1, gram(whl, whl))
     nk = cores_start(n12, 2, nc)
-    wait_all(py)
-    res[three(x, y), up_rows] = part[three(x, y), up_rows] + ((yr[0, 0] + yr[0, 1]) + yr[0, 2])
-    res[three(y, x), down_rows] = part[three(y, x), down_rows] + ((yr[1, 0] + yr[1, 1]) + yr[1, 2])
-    own_a, own_b = res.at[three(x, y), up_rows], res.at[three(y, x), down_rows]
-    ry = to_three(lambda d: own_a, lambda d: own_a, dev_y) + to_three(lambda d: own_b, lambda d: own_b, dev_x)
-    wk.wait_recv()
-
-    def second_image(i, total):
-        value = cov_times(i, whl)
-        return total + dot_t(wr[i].reshape(336, E), value)
-
-    total = lax.fori_loop(0, 2, second_image, jnp.zeros((E, E), F32))
+    axis_end(n3z, n3, 1, n3r.at[0], n3.at[pl.ds(1, 1)])
+    n3y = axis_start(n3.at[pl.ds(1, 1)], 1, n3r.at[1], dev_y)
     cores_end(nk, n12, 2, nc)
     nz = axis_start(n12, 2, nzr, dev_z)
-    wait_all(ry)
-    own_a, own_b = res.at[twelve(x), up_rows], res.at[twelve(y), down_rows]
-    rx = to_three(lambda d: own_a, lambda d: own_a, dev_x) + to_three(lambda d: own_b, lambda d: own_b, dev_y)
-    total = lax.fori_loop(2, 4, second_image, total)
-    halve(n3, 0, total)
-    n3k = cores_start(n3, 1, mc2)
+    wait_all(rx)
+    own_z = res.at[real, own_rows]
+    rz = to_three(lambda d: own_z, lambda d: own_z, dev_z)
+    axis_end(n3y, n3.at[pl.ds(1, 1)], 1, n3r.at[1], n3.at[pl.ds(2, 1)])
+    n3x = axis_start(n3.at[pl.ds(2, 1)], 1, n3r.at[2], dev_x)
     axis_end(nz, n12, 2, nzr, gsum.at[pl.ds(1, 2)])
     gs = cores_share(gsum)
-    wait_all(rx)
-    own_z = res.at[real, pl.ds(pl.multiple_of(k * 64 + z * 16, 8), 16)]
-    rz = [cp(own_z, own_z, dev_z(1)), cp(own_z, own_z, dev_z(3))]
-    cores_end(n3k, n3, 1, mc2)
-    n3y = axis_start(n3, 1, n3r.at[0], dev_y)
     gs.wait_recv()
 
     def whole(ref, i):
@@ -448,21 +416,10 @@
     gram0, n1, n2 = sym(whole(gsum, 0)), sym(whole(gsum, 1)), sym(whole(gsum, 2))
     square = dot(gram0, gram0)
     m1 = sym(n1 + square)
-    axis_end(n3y, n3, 1, n3r.at[0], n3.at[pl.ds(1, 1)])
-    n3x = axis_start(n3.at[pl.ds(1, 1)], 1, n3r.at[1], dev_x)
     inv0, inv1 = sweep_some(5, gram0, m1)
-    axis_end(n3x, n3.at[pl.ds(1, 1)], 1, n3r.at[1], n3.at[pl.ds(2, 1)])
-    n3z = axis_start(n3.at[pl.ds(2, 1)], 1, n3r.at[2], dev_z)
-    inv0, inv1 = sweep_some(6, inv0, inv1)
-    rz[0].wait_recv()
-    fwd0 = res.at[real, rows_of((z + 3) % 4, 0)]
-    rf0 = cp(fwd0, fwd0, dev_z(1))
-    rz[1].wait_recv()
-    fwd1 = res.at[real, rows_of((z + 1) % 4, 1)]
-    rf1 = cp(fwd1, fwd1, dev_z(3))
-    axis_end(n3z, n3.at[pl.ds(2, 1)], 1, n3r.at[2], n3.at[pl.ds(3, 1)])
+    axis_end(n3x, n3.at[pl.ds(2, 1)], 1, n3r.at[2], n3.at[pl.ds(3, 1)])
     n3s = cores_share(n3.at[pl.ds(3, 1)])
-    inv0, inv1 = sweep_some(5, inv0, inv1)
+    inv0, inv1 = sweep_some(11, inv0, inv1)
     n1m0 = dot(n1, gram0)
     m2 = sym(n2 + n1m0 + n1m0.T + dot(square, gram0))
     n2m0 = dot(n2, gram0)
@@ -479,7 +436,7 @@
     n3s.wait_recv()
     m3 = m3_rest + sym(whole(n3, 3))
     curvature = sym(curv_rest + dot_t(alpha0, dot(m3, alpha0)))
-    wait_all([rf0, rf1])
+    wait_all(rz)
     half = res.at[real, half_of(k)]
     rkk = cp(half, half, dev_k)
     (inv2,) = sweep_some(16, curvature)
@@ -522,15 +479,12 @@
             pltpu.VMEM((336, 2688), BF16),
             pltpu.VMEM((PIECE, D), BF16),
             small(2, LINES, E),
-            small(2688, 2 * E),
             small(2, 4, 4, PIECE, E),
             small(2, 4, 4, PIECE, E),
             small(2, 2, 4, PIECE, E),
             small(2, 2, 4, PIECE, E),
             small(2, 2, 4, PIECE, E),
-            small(2, 2, PIECE, E),
-            small(2, 2, PIECE, E),
-            small(2, 2, PIECE, E),
+            small(2, 3, 2, PIECE, E),
             pltpu.VMEM((1344, 2688), BF16),
             pltpu.VMEM((1344, 2688), BF16),
             small(2, PIECE, E),
@@ -540,17 +494,12 @@
             pltpu.VMEM((2688, 2 * E), BF16),
             small(4, 2, PIECE, E),
             small(4, PIECE, E),
-            small(2, 88, E),
-            small(2, 88, E),
-            small(2, 88, E),
+            small(3, PIECE, E),
             small(4, 2, PIECE, E),
             small(48, E, E),
             small(42, 64, E),
-            small(2, 42, 8, E),
-            small(2, 42, 8, E),
-            small(2, 42, 8, E),
-            small(2, 3, 12, 8, E),
-            small(2, 3, 3, 8, E),
+            small(3, 42, 16, E),
+            small(15, 3, 16, E),
             small(48, E, E),
             small(48, E),
             small(1, 2, 64, E),

time: 149 us -> 152 us (1.020)
  the two profiles are of different devices: /device:TPU:1 before, /device:TPU:97 now
where the time goes in v3:
time: 152 us
  Pallas kernels  149 us (98%)
  local copies, waits for them, and re-layouts  2.83 us (2%)
    pallas_call x1, Pallas kernels, body(): pl.pallas_call(kernel, out_shape=jax.ShapeDtypeStruct((PIECE, D), BF16),...  149 us

profile of v3, /device:TPU:97, one launch (start us, length us, event | category | flops | bytes accessed | tf_op | source)
XLA Modules:
  0.0 151.7 jit_solution(5761770364107395964)
XLA Ops:
  0.0 148.9 %edit.1 = bf16[168,5376]{1,0:T(8,128)(2,1)} custom-call(bf16[2,8,336,128]{3,2,1,0:T(8,128)(2,1)} %bitcast.12, s32[2,128]{1,0:T(2,128)} %bitcast.13, bf16[336,2688]{1,0:T(8,128)(2,1)} %bitcast.9, bf16[336,2688]{1,0:T(8,128)(2,1)} %bitcast.10, bf16[168,5376]{1,0:T(8,128)(2,1)} %bitcast.11, f32[28224,128]{1,0:T(8,128)} %bitcast.7, f32[42,128]{1,0:T(8,128)} %tgt.1), custom_call_target="tpu_custom_call" | custom-call | tf_op jit(solution)/shard_map/edit/pallas_call | solution.py:471
  148.9 2.8 %copy.9 = bf16[1,1,168,5376]{3,2,1,0:T(8,128)(2,1)} copy(bf16[1,1,168,5376]{3,2,1,0:T(8,128)(2,1)} %bitcast.8) | data formatting | bytes 3612672

commit v4 on v3

--- a/solution.py
+++ b/solution.py
@@ -46,18 +46,25 @@
 
 
 def sweep_panel(matrix):
-    lane = lax.broadcasted_iota(jnp.int32, (E, E), 1)
-    sub = lax.broadcasted_iota(jnp.int32, (E, E), 0)
+    lane8 = lax.broadcasted_iota(jnp.int32, (8, E), 1)
+    sub8 = lax.broadcasted_iota(jnp.int32, (8, E), 0)
+    lane = lax.broadcasted_iota(jnp.int32, (E - 8, E), 1)
     lane1 = lax.broadcasted_iota(jnp.int32, (1, E), 1)
-    for j in range(8):
-        column = matrix[:, j : j + 1]
-        row = matrix[j : j + 1, :]
-        inv = 1.0 / matrix[j : j + 1, j : j + 1]
-        row = jnp.where(lane1 == j, inv, row * inv)
-        rest = jnp.where(lane == j, 0.0, matrix) - column * row
-        matrix = jnp.where(sub == j, row, rest)
-    matrix = jnp.concatenate([matrix[8:], matrix[:8]], axis=0)
-    return pltpu.roll(matrix, E - 8, 1)
+    top, rest = matrix[:8], matrix[8:]
+    for base in (0, 4):
+        tops = [jnp.broadcast_to(top[:, base + j : base + j + 1], (8, E)) for j in range(4)]
+        rests = [jnp.broadcast_to(rest[:, base + j : base + j + 1], (E - 8, E)) for j in range(4)]
+        for j in range(4):
+            r = base + j
+            inv = 1.0 / tops[j][r : r + 1, :]
+            row = jnp.where(lane1 == r, inv, top[r : r + 1, :] * inv)
+            rest = jnp.where(lane == r, 0.0, rest) - rests[j] * row
+            top = jnp.where(sub8 == r, row, jnp.where(lane8 == r, 0.0, top) - tops[j] * row)
+            for m in range(j + 1, 4):
+                factor = tops[m][r : r + 1, :] * inv
+                rests[m] = rests[m] - rests[j] * factor
+                tops[m] = jnp.where(sub8 == r, factor, tops[m] - tops[j] * factor)
+    return pltpu.roll(jnp.concatenate([rest, top], axis=0), E - 8, 1)
 
 
 def sweep_some(count, *matrices):
@@ -376,13 +383,19 @@
     axis_end(mz, m0, 1, mzr, gsum)
     wait_all(wg)
     split_field(wc, whl)
+    halve(n12, 0, gram(bhl, whl))
+    first_n = n12.at[pl.ds(0, 1)]
+    nk = cores_start(first_n, 1, nc.at[pl.ds(0, 1)])
     wk.wait_recv()
 
     def second_image(i, total):
         value = cov_times(i, whl)
         return total + dot_t(wr[i].reshape(336, E), value)
 
-    total = lax.fori_loop(0, 4, second_image, jnp.zeros((E, E), F32))
+    total = lax.fori_loop(0, 2, second_image, jnp.zeros((E, E), F32))
+    cores_end(nk, first_n, 1, nc.at[pl.ds(0, 1)])
+    nz = axis_start(first_n, 1, nzr.at[0], dev_z)
+    total = lax.fori_loop(2, 4, second_image, total)
     halve(n3, 0, total)
     n3k = cores_start(n3, 1, mc2)
     wait_all(px)
@@ -391,60 +404,52 @@
         mine = mine + xr[n]
     res[three(x, y), own_rows] = mine
     own = res.at[three(x, y), own_rows]
-    rx = [cp(own, own, dev_xy(i, j)) for i, j in others]
     cores_end(n3k, n3, 1, mc2)
     n3z = axis_start(n3, 1, n3r.at[0], dev_z)
-    halve(n12, 0, gram(bhl, whl))
+    axis_end(nz, first_n, 1, nzr.at[0], gsum.at[pl.ds(1, 1)])
+    gs = cores_share(gsum.at[pl.ds(0, 2)])
+    rx = [cp(own, own, dev_xy(i, j)) for i, j in others]
     halve(n12, 1, gram(whl, whl))
-    nk = cores_start(n12, 2, nc)
+    second_n = n12.at[pl.ds(1, 1)]
+    nk = cores_start(second_n, 1, nc.at[pl.ds(1, 1)])
+    gs.wait_recv()
+
+    def whole(ref, i):
+        return jnp.concatenate([ref[i, 0], ref[i, 1]], axis=0)
+
+    gram0, n1 = sym(whole(gsum, 0)), sym(whole(gsum, 1))
+    g11 = sym(n1 + dot(gram0, gram0))
+    (inv1,) = sweep_some(2, g11)
     axis_end(n3z, n3, 1, n3r.at[0], n3.at[pl.ds(1, 1)])
     n3y = axis_start(n3.at[pl.ds(1, 1)], 1, n3r.at[1], dev_y)
-    cores_end(nk, n12, 2, nc)
-    nz = axis_start(n12, 2, nzr, dev_z)
+    cores_end(nk, second_n, 1, nc.at[pl.ds(1, 1)])
+    nz = axis_start(second_n, 1, nzr.at[1], dev_z)
+    (inv1,) = sweep_some(6, inv1)
+    axis_end(n3y, n3.at[pl.ds(1, 1)], 1, n3r.at[1], n3.at[pl.ds(2, 1)])
+    n3x = axis_start(n3.at[pl.ds(2, 1)], 1, n3r.at[2], dev_x)
+    axis_end(nz, second_n, 1, nzr.at[1], gsum.at[pl.ds(2, 1)])
+    gs = cores_share(gsum.at[pl.ds(2, 1)])
     wait_all(rx)
     own_z = res.at[real, own_rows]
     rz = to_three(lambda d: own_z, lambda d: own_z, dev_z)
-    axis_end(n3y, n3.at[pl.ds(1, 1)], 1, n3r.at[1], n3.at[pl.ds(2, 1)])
-    n3x = axis_start(n3.at[pl.ds(2, 1)], 1, n3r.at[2], dev_x)
-    axis_end(nz, n12, 2, nzr, gsum.at[pl.ds(1, 2)])
-    gs = cores_share(gsum)
-    gs.wait_recv()
-
-    def whole(ref, i):
-        return jnp.concatenate([ref[i, 0], ref[i, 1]], axis=0)
-
-    gram0, n1, n2 = sym(whole(gsum, 0)), sym(whole(gsum, 1)), sym(whole(gsum, 2))
-    square = dot(gram0, gram0)
-    m1 = sym(n1 + square)
-    inv0, inv1 = sweep_some(5, gram0, m1)
+    (inv1,) = sweep_some(8, inv1)
     axis_end(n3x, n3.at[pl.ds(2, 1)], 1, n3r.at[2], n3.at[pl.ds(3, 1)])
     n3s = cores_share(n3.at[pl.ds(3, 1)])
-    inv0, inv1 = sweep_some(11, inv0, inv1)
-    n1m0 = dot(n1, gram0)
-    m2 = sym(n2 + n1m0 + n1m0.T + dot(square, gram0))
-    n2m0 = dot(n2, gram0)
-    m3_rest = sym(n2m0 + n2m0.T + dot(gram0, n1m0) + dot(m1, m1))
-    alpha0 = dot(inv1, gram0)
-    norm1 = sym(dot_t(alpha0, dot(m2, alpha0)) - gram0)
-    beta = dot(inv0, norm1)
-    eye = jnp.where(
-        lax.broadcasted_iota(jnp.int32, (E, E), 0) == lax.broadcasted_iota(jnp.int32, (E, E), 1), 1.0, 0.0
-    )
-    c1 = eye + beta
-    cross = dot_t(c1, dot(m2, alpha0))
-    curv_rest = dot_t(c1, dot(m1, c1)) - cross - cross.T
+    gs.wait_recv()
+    g12 = sym(whole(gsum, 2)) + dot(gram0, n1)
+    solved = dot(inv1, jnp.concatenate([g12, gram0], axis=1))
+    taken = dot_t(g12, solved)
+    g22 = dot(n1, n1)
     n3s.wait_recv()
-    m3 = m3_rest + sym(whole(n3, 3))
-    curvature = sym(curv_rest + dot_t(alpha0, dot(m3, alpha0)))
+    schur = sym(sym(whole(n3, 3)) + g22 - taken[:, :E])
+    right2 = n1 - taken[:, E:]
     wait_all(rz)
     half = res.at[real, half_of(k)]
     rkk = cp(half, half, dev_k)
-    (inv2,) = sweep_some(16, curvature)
-    alpha1 = dot(inv2, norm1)
-    on_w = -dot(alpha0, alpha1)
-    tmp[0] = dot(c1, alpha1)
-    tmp[1] = dot(gram0, on_w)
-    on_b = alpha0 + (tmp[0] + tmp[1])
+    (inv2,) = sweep_some(16, schur)
+    on_w = dot(inv2, right2)
+    tmp[0] = dot(solved[:, :E], on_w)
+    on_b = solved[:, E:] - tmp[0]
     fh, fl = halves(jnp.concatenate([piece[0], piece[1]], axis=1))
     ch, cl = halves(jnp.concatenate([on_b, on_w], axis=0))
     found = dot_b(fh, ch) + (dot_b(fh, cl) + dot_b(fl, ch))
@@ -459,7 +464,7 @@
         out[:, pl.ds(pl.multiple_of(j * 256, 128), 256)] = value.astype(BF16)
         return carry
 
-    lax.fori_loop(0, 21, update, 0)
+    lax.fori_loop(0, 21, update, 0, unroll=3)
     for copy in sent:
         copy.wait_send()
 
@@ -509,10 +514,10 @@
             small(2, 64, E),
             small(1, 64, E),
             small(3, 1, 64, E),
-            small(3, 2, 64, E),
+            small(2, 3, 1, 64, E),
             small(3, 3, 1, 64, E),
             small(3, 2, 64, E),
-            small(2, E, E),
+            small(1, E, E),
             pltpu.SemaphoreType.DMA((N_SEM,)),
             pltpu.SemaphoreType.DMA((N_SEM,)),
             pltpu.SemaphoreType.DMA((6,)),

time: 152 us -> 140 us (0.921)
  the two profiles are of different devices: /device:TPU:97 before, /device:TPU:1 now
where the time goes in v4:
time: 140 us; the launch traced here: 139 us
  Pallas kernels  136 us (97%)
  local copies, waits for them, and re-layouts  2.83 us (2%)
    pallas_call x1, Pallas kernels, body(): pl.pallas_call(kernel, out_shape=jax.ShapeDtypeStruct((PIECE, D), BF16),...  136 us
    unnamed x1, local copies, waits for them, and re-layouts  2.83 us

profile of v4, /device:TPU:1, one launch (start us, length us, event | category | flops | bytes accessed | tf_op | source)
XLA Modules:
  0.0 139.3 jit_solution(1652751618534103416)
XLA Ops:
  0.0 136.5 %edit.1 = bf16[168,5376]{1,0:T(8,128)(2,1)} custom-call(bf16[2,8,336,128]{3,2,1,0:T(8,128)(2,1)} %bitcast.12, s32[2,128]{1,0:T(2,128)} %bitcast.13, bf16[336,2688]{1,0:T(8,128)(2,1)} %bitcast.9, bf16[336,2688]{1,0:T(8,128)(2,1)} %bitcast.10, bf16[168,5376]{1,0:T(8,128)(2,1)} %bitcast.11, f32[28224,128]{1,0:T(8,128)} %bitcast.7, f32[42,128]{1,0:T(8,128)} %tgt.1), custom_call_target="tpu_custom_call" | custom-call | tf_op jit(solution)/shard_map/edit/pallas_call | solution.py:476
  136.5 2.8 %copy.9 = bf16[1,1,168,5376]{3,2,1,0:T(8,128)(2,1)} copy(bf16[1,1,168,5376]{3,2,1,0:T(8,128)(2,1)} %bitcast.8) | data formatting | bytes 3612672

commit v5 on v4

--- a/solution.py
+++ b/solution.py
@@ -129,7 +129,6 @@
     peers += [dev_xy(i, j) for i, j in others]
     for peer in peers:
         pl.semaphore_signal(barrier, inc=1, device_id=peer, device_id_type=pl.DeviceIdType.MESH)
-    pl.semaphore_wait(barrier, len(peers))
 
     def ring_far(data, ra, me, dev):
         m2 = (me + 2) % 4
@@ -210,18 +209,19 @@
 
     loads[1].wait()
     project(gw, gate, False)
+    pl.semaphore_wait(barrier, len(peers))
     g_far = ring_far(gate_data, buf(ra1, 0), x, dev_x)
     loads[2].wait()
     project(uw, up, True)
     u_far = ring_far(up_data, buf(ra1, 1), y, dev_y)
+    lax.fori_loop(0, 6, cov_step, 0)
     g_near = ring_near(gate_data, buf(rb1, 0), x, dev_x)
-    lax.fori_loop(0, 3, cov_step, 0)
+    lax.fori_loop(6, 7, cov_step, 0)
     u_near = ring_near(up_data, buf(rb1, 1), y, dev_y)
-    lax.fori_loop(3, 6, cov_step, 0)
+    lax.fori_loop(7, 10, cov_step, 0)
     g_near += ring_middle(g_far, gate_data, buf(ra1, 0), buf(rc1, 0), x, dev_x)
-    lax.fori_loop(6, 8, cov_step, 0)
     u_near += ring_middle(u_far, up_data, buf(ra1, 1), buf(rc1, 1), y, dev_y)
-    lax.fori_loop(8, COV_STEPS, cov_step, 0)
+    lax.fori_loop(10, COV_STEPS, cov_step, 0)
     ring_end(g_near, gate_data, buf(rb1, 0), buf(rc1, 0), x)
     g2 = to_three(lambda d: gate.at[:, x, (y + d) % 4], lambda d: ra2.at[0, d - 1], dev_y)
     ring_end(u_near, up_data, buf(rb1, 1), buf(rc1, 1), y)
@@ -354,20 +354,11 @@
 
     lax.fori_loop(0, 4, first_image, 0)
     v1 = cp(vv.at[:, 1 - k], vk, dev_k)
+    v1.wait_recv()
+    vv[:, k] += vk[...]
+    vz = to_three(lambda d: vv.at[(z + d) % 4, k], lambda d: va.at[d - 1], dev_z)
     halve(m0, 0, gram(bhl, bhl))
     mk = cores_start(m0, 1, mc)
-    v1.wait_recv()
-    vv[:, k] += vk[...]
-
-    vz = to_three(lambda d: vv.at[(z + d) % 4, k], lambda d: va.at[d - 1], dev_z)
-    cores_end(mk, m0, 1, mc)
-    wait_all(vz)
-    piece[1] = vv[z, k] + ((va[0] + va[1]) + va[2])
-    wg = gather_start(wc, 1)
-    wr[z, k] = piece[1]
-    wz = to_three(lambda d: wr.at[z, k], lambda d: wr.at[z, k], dev_z)
-    mz = axis_start(m0, 1, mzr, dev_z)
-    wg = gather_next(wg, wc)
 
     def three(xx, yy):
         return pl.ds(xx * 12 + yy * 3, 3)
@@ -378,6 +369,21 @@
         cp(part.at[three((x + i) % 4, (y + j) % 4), own_rows], xr.at[n], dev_xy(i, j))
         for n, (i, j) in enumerate(others)
     ]
+    wait_all(vz)
+    piece[1] = vv[z, k] + ((va[0] + va[1]) + va[2])
+    wg = gather_start(wc, 1)
+    wr[z, k] = piece[1]
+    wz = to_three(lambda d: wr.at[z, k], lambda d: wr.at[z, k], dev_z)
+    cores_end(mk, m0, 1, mc)
+    mz = axis_start(m0, 1, mzr, dev_z)
+    wg = gather_next(wg, wc)
+    wait_all(px)
+    mine = part[three(x, y), own_rows]
+    for n in range(15):
+        mine = mine + xr[n]
+    res[three(x, y), own_rows] = mine
+    own = res.at[three(x, y), own_rows]
+    rx = [cp(own, own, dev_xy(i, j)) for i, j in others]
     wait_all(wz)
     wk = cp(wr.at[:, k], wr.at[:, k], dev_k)
     axis_end(mz, m0, 1, mzr, gsum)
@@ -395,20 +401,16 @@
     total = lax.fori_loop(0, 2, second_image, jnp.zeros((E, E), F32))
     cores_end(nk, first_n, 1, nc.at[pl.ds(0, 1)])
     nz = axis_start(first_n, 1, nzr.at[0], dev_z)
+    wait_all(rx)
+    own_z = res.at[real, own_rows]
+    rz = to_three(lambda d: own_z, lambda d: own_z, dev_z)
     total = lax.fori_loop(2, 4, second_image, total)
     halve(n3, 0, total)
     n3k = cores_start(n3, 1, mc2)
-    wait_all(px)
-    mine = part[three(x, y), own_rows]
-    for n in range(15):
-        mine = mine + xr[n]
-    res[three(x, y), own_rows] = mine
-    own = res.at[three(x, y), own_rows]
     cores_end(n3k, n3, 1, mc2)
     n3z = axis_start(n3, 1, n3r.at[0], dev_z)
     axis_end(nz, first_n, 1, nzr.at[0], gsum.at[pl.ds(1, 1)])
     gs = cores_share(gsum.at[pl.ds(0, 2)])
-    rx = [cp(own, own, dev_xy(i, j)) for i, j in others]
     halve(n12, 1, gram(whl, whl))
     second_n = n12.at[pl.ds(1, 1)]
     nk = cores_start(second_n, 1, nc.at[pl.ds(1, 1)])
@@ -429,9 +431,6 @@
     n3x = axis_start(n3.at[pl.ds(2, 1)], 1, n3r.at[2], dev_x)
     axis_end(nz, second_n, 1, nzr.at[1], gsum.at[pl.ds(2, 1)])
     gs = cores_share(gsum.at[pl.ds(2, 1)])
-    wait_all(rx)
-    own_z = res.at[real, own_rows]
-    rz = to_three(lambda d: own_z, lambda d: own_z, dev_z)
     (inv1,) = sweep_some(8, inv1)
     axis_end(n3x, n3.at[pl.ds(2, 1)], 1, n3r.at[2], n3.at[pl.ds(3, 1)])
     n3s = cores_share(n3.at[pl.ds(3, 1)])

time: 140 us -> 139 us (level)
  no operation moved by 1% of the time
where the time goes in v5:
time: 139 us
  Pallas kernels  136 us (98%)
  local copies, waits for them, and re-layouts  2.83 us (2%)
    pallas_call x1, Pallas kernels, body(): pl.pallas_call(kernel, out_shape=jax.ShapeDtypeStruct((PIECE, D), BF16),...  136 us
    unnamed x1, local copies, waits for them, and re-layouts  2.83 us

profile of v5, /device:TPU:1, one launch (start us, length us, event | category | flops | bytes accessed | tf_op | source)
XLA Modules:
  0.0 138.6 jit_solution(14258393456988390626)
XLA Ops:
  0.0 135.7 %edit.1 = bf16[168,5376]{1,0:T(8,128)(2,1)} custom-call(bf16[2,8,336,128]{3,2,1,0:T(8,128)(2,1)} %bitcast.12, s32[2,128]{1,0:T(2,128)} %bitcast.13, bf16[336,2688]{1,0:T(8,128)(2,1)} %bitcast.9, bf16[336,2688]{1,0:T(8,128)(2,1)} %bitcast.10, bf16[168,5376]{1,0:T(8,128)(2,1)} %bitcast.11, f32[28224,128]{1,0:T(8,128)} %bitcast.7, f32[42,128]{1,0:T(8,128)} %tgt.1), custom_call_target="tpu_custom_call" | custom-call | tf_op jit(solution)/shard_map/edit/pallas_call | solution.py:475
  135.7 2.8 %copy.9 = bf16[1,1,168,5376]{3,2,1,0:T(8,128)(2,1)} copy(bf16[1,1,168,5376]{3,2,1,0:T(8,128)(2,1)} %bitcast.8) | data formatting | bytes 3612672

commit v6 on v5

--- a/solution.py
+++ b/solution.py
@@ -76,7 +76,7 @@
     out,
     states, gw, uw, dw, cbuf, gate, up, ra1, rb1, rc1, ra2,
     chi, clo, piece, bc, wc, bhl, whl, vv, vk, va, wr,
-    part, rk, pa, xr, res, tp, m0, n12, n3, mc, nc, mc2, mzr, nzr, n3r, gsum, tmp, send, recv, local,
+    part, rk, xr, yr, zr, res, tp, m0, n12, n3, mc, nc, mc2, mzr, nzr, n3r, gsum, tmp, send, recv, local,
 ):
     a = lax.axis_index("row")
     b = lax.axis_index("col")
@@ -91,11 +91,6 @@
 
     def dev_z(d):
         return {"col": ((z + d) % 4) * 2 + k}
-
-    others = [(i, j) for i in range(4) for j in range(4) if i + j > 0]
-
-    def dev_xy(i, j):
-        return {"row": ((x + i) % 4) * 4 + (y + j) % 4}
 
     dev_k = {"col": z * 2 + 1 - k}
     sent = []
@@ -125,8 +120,7 @@
     cov_load(0, 0).start()
 
     barrier = pltpu.get_barrier_semaphore()
-    peers = [dev_z(d) for d in (1, 2, 3)] + [dev_k]
-    peers += [dev_xy(i, j) for i, j in others]
+    peers = [dev(d) for dev in (dev_x, dev_y, dev_z) for d in (1, 2, 3)] + [dev_k]
     for peer in peers:
         pl.semaphore_signal(barrier, inc=1, device_id=peer, device_id_type=pl.DeviceIdType.MESH)
 
@@ -308,8 +302,22 @@
     def half_of(kk):
         return pl.ds(pl.multiple_of(kk * 64, 8), 64)
 
-    def rows_of(zz):
-        return pl.ds(pl.multiple_of(k * 64 + zz * 16, 8), 16)
+    def rows_h(h):
+        return pl.ds(pl.multiple_of(k * 64 + h * 32, 8), 32)
+
+    def rows_z(h):
+        return pl.ds(pl.multiple_of(k * 64 + h * 32 + z * 8, 8), 8)
+
+    def rows_to(h, d):
+        return pl.ds(pl.multiple_of(k * 64 + h * 32 + ((z + d) % 4) * 8, 8), 8)
+
+    def twelve(t):
+        return pl.ds(t * 12, 12)
+
+    def three(t, u):
+        return pl.ds(t * 12 + u * 3, 3)
+
+    ways = ((0, x, dev_x, y, dev_y), (1, y, dev_y, x, dev_x))
 
     p1 = cp(part.at[real, half_of(1 - k)], rk, dev_k)
     bg = gather_next(bg, bc)
@@ -320,8 +328,9 @@
         return carry
 
     lax.fori_loop(0, 42, add_half, 0)
-    own_rows = rows_of(z)
-    pz = to_three(lambda d: part.at[real, rows_of((z + d) % 4)], lambda d: pa.at[d - 1], dev_z)
+    px = []
+    for h, u, dev_u, _, _ in ways:
+        px += to_three(lambda d: part.at[twelve((u + d) % 4), rows_h(h)], lambda d: xr.at[h, d - 1], dev_u)
     wait_all(bg)
     split_field(bc, bhl)
 
@@ -357,41 +366,50 @@
     v1.wait_recv()
     vv[:, k] += vk[...]
     vz = to_three(lambda d: vv.at[(z + d) % 4, k], lambda d: va.at[d - 1], dev_z)
+    wait_all(px)
+    py = []
+    for h, u, _, w, dev_w in ways:
+        part[twelve(u), rows_h(h)] += (xr[h, 0] + xr[h, 1]) + xr[h, 2]
+        py += to_three(lambda d: part.at[three(u, (w + d) % 4), rows_h(h)], lambda d: yr.at[h, d - 1], dev_w)
     halve(m0, 0, gram(bhl, bhl))
     mk = cores_start(m0, 1, mc)
-
-    def three(xx, yy):
-        return pl.ds(xx * 12 + yy * 3, 3)
-
-    wait_all(pz)
-    part[real, own_rows] += (pa[0] + pa[1]) + pa[2]
-    px = [
-        cp(part.at[three((x + i) % 4, (y + j) % 4), own_rows], xr.at[n], dev_xy(i, j))
-        for n, (i, j) in enumerate(others)
-    ]
     wait_all(vz)
     piece[1] = vv[z, k] + ((va[0] + va[1]) + va[2])
     wg = gather_start(wc, 1)
     wr[z, k] = piece[1]
     wz = to_three(lambda d: wr.at[z, k], lambda d: wr.at[z, k], dev_z)
+    wait_all(py)
+    pz = []
+    for h, u, _, w, _ in ways:
+        part[three(u, w), rows_h(h)] += (yr[h, 0] + yr[h, 1]) + yr[h, 2]
+        pz += to_three(lambda d: part.at[three(u, w), rows_to(h, d)], lambda d: zr.at[h, d - 1], dev_z)
     cores_end(mk, m0, 1, mc)
     mz = axis_start(m0, 1, mzr, dev_z)
     wg = gather_next(wg, wc)
-    wait_all(px)
-    mine = part[three(x, y), own_rows]
-    for n in range(15):
-        mine = mine + xr[n]
-    res[three(x, y), own_rows] = mine
-    own = res.at[three(x, y), own_rows]
-    rx = [cp(own, own, dev_xy(i, j)) for i, j in others]
+    wait_all(pz)
+    rz = []
+    for h, u, _, w, _ in ways:
+        res[three(u, w), rows_z(h)] = part[three(u, w), rows_z(h)] + ((zr[h, 0] + zr[h, 1]) + zr[h, 2])
+        mine = res.at[three(u, w), rows_z(h)]
+        rz += to_three(lambda d: mine, lambda d: mine, dev_z)
     wait_all(wz)
     wk = cp(wr.at[:, k], wr.at[:, k], dev_k)
     axis_end(mz, m0, 1, mzr, gsum)
+    wait_all(rz)
+    ry = []
+    for h, u, _, w, dev_w in ways:
+        block = res.at[three(u, w), rows_h(h)]
+        ry += to_three(lambda d: block, lambda d: block, dev_w)
     wait_all(wg)
     split_field(wc, whl)
     halve(n12, 0, gram(bhl, whl))
     first_n = n12.at[pl.ds(0, 1)]
     nk = cores_start(first_n, 1, nc.at[pl.ds(0, 1)])
+    wait_all(ry)
+    rx = []
+    for h, u, dev_u, _, _ in ways:
+        lines = res.at[twelve(u), rows_h(h)]
+        rx += to_three(lambda d: lines, lambda d: lines, dev_u)
     wk.wait_recv()
 
     def second_image(i, total):
@@ -401,9 +419,6 @@
     total = lax.fori_loop(0, 2, second_image, jnp.zeros((E, E), F32))
     cores_end(nk, first_n, 1, nc.at[pl.ds(0, 1)])
     nz = axis_start(first_n, 1, nzr.at[0], dev_z)
-    wait_all(rx)
-    own_z = res.at[real, own_rows]
-    rz = to_three(lambda d: own_z, lambda d: own_z, dev_z)
     total = lax.fori_loop(2, 4, second_image, total)
     halve(n3, 0, total)
     n3k = cores_start(n3, 1, mc2)
@@ -431,6 +446,9 @@
     n3x = axis_start(n3.at[pl.ds(2, 1)], 1, n3r.at[2], dev_x)
     axis_end(nz, second_n, 1, nzr.at[1], gsum.at[pl.ds(2, 1)])
     gs = cores_share(gsum.at[pl.ds(2, 1)])
+    wait_all(rx)
+    half = res.at[real, half_of(k)]
+    rkk = cp(half, half, dev_k)
     (inv1,) = sweep_some(8, inv1)
     axis_end(n3x, n3.at[pl.ds(2, 1)], 1, n3r.at[2], n3.at[pl.ds(3, 1)])
     n3s = cores_share(n3.at[pl.ds(3, 1)])
@@ -442,9 +460,6 @@
     n3s.wait_recv()
     schur = sym(sym(whole(n3, 3)) + g22 - taken[:, :E])
     right2 = n1 - taken[:, E:]
-    wait_all(rz)
-    half = res.at[real, half_of(k)]
-    rkk = cp(half, half, dev_k)
     (inv2,) = sweep_some(16, schur)
     on_w = dot(inv2, right2)
     tmp[0] = dot(solved[:, :E], on_w)
@@ -502,8 +517,9 @@
             small(4, 2, PIECE, E),
             small(48, E, E),
             small(42, 64, E),
-            small(3, 42, 16, E),
-            small(15, 3, 16, E),
+            small(2, 3, 12, 32, E),
+            small(2, 3, 3, 32, E),
+            small(2, 3, 3, 8, E),
             small(48, E, E),
             small(48, E),
             small(1, 2, 64, E),

time: 139 us -> 125 us (0.90)
  Pallas kernels: 136 us -> 122 us
    pallas_call x1, Pallas kernels: 136 us -> 122 us  [body(): pl.pallas_call(kernel, out_shape=jax.ShapeDtypeStruct((PIECE, D), BF16),...]
where the time goes in v6:
time: 125 us
  Pallas kernels  122 us (98%)
  local copies, waits for them, and re-layouts  2.83 us (2%)
    pallas_call x1, Pallas kernels, body(): pl.pallas_call(kernel, out_shape=jax.ShapeDtypeStruct((PIECE, D), BF16),...  122 us
    unnamed x1, local copies, waits for them, and re-layouts  2.83 us

profile of v6, /device:TPU:1, one launch (start us, length us, event | category | flops | bytes accessed | tf_op | source)
XLA Modules:
  0.0 124.6 jit_solution(10923289383236220093)
XLA Ops:
  0.0 121.8 %edit.1 = bf16[168,5376]{1,0:T(8,128)(2,1)} custom-call(bf16[2,8,336,128]{3,2,1,0:T(8,128)(2,1)} %bitcast.12, s32[2,128]{1,0:T(2,128)} %bitcast.13, bf16[336,2688]{1,0:T(8,128)(2,1)} %bitcast.9, bf16[336,2688]{1,0:T(8,128)(2,1)} %bitcast.10, bf16[168,5376]{1,0:T(8,128)(2,1)} %bitcast.11, f32[28224,128]{1,0:T(8,128)} %bitcast.7, f32[42,128]{1,0:T(8,128)} %tgt.1), custom_call_target="tpu_custom_call" | custom-call | tf_op jit(solution)/shard_map/edit/pallas_call | solution.py:490
  121.8 2.8 %copy.9 = bf16[1,1,168,5376]{3,2,1,0:T(8,128)(2,1)} copy(bf16[1,1,168,5376]{3,2,1,0:T(8,128)(2,1)} %bitcast.8) | data formatting | bytes 3612672

commit v7 on v6

--- a/solution.py
+++ b/solution.py
@@ -14,7 +14,7 @@
 F32 = jnp.float32
 BF16 = jnp.bfloat16
 HI = lax.Precision.HIGHEST
-N_SEM = 180
+N_SEM = 220
 COV_ROWS = 112
 COV_STEPS = 1344 // COV_ROWS
 LINES = COV_ROWS * 21
@@ -177,14 +177,16 @@
                 target[1, first, second, off : off + size] = lines[:, E:]
                 row += size
 
-    def gate_data(h, t):
-        return gate.at[h, t]
-
-    def up_data(h, t):
-        return up.at[h, t]
-
-    def buf(ref, which):
-        return lambda h: ref.at[which, h]
+    cuts = (pl.ds(0, 88), pl.ds(88, 80))
+
+    def gate_data(q):
+        return lambda h, t: gate.at[h, t, :, cuts[q]]
+
+    def up_data(q):
+        return lambda h, t: up.at[h, t, :, cuts[q]]
+
+    def buf(ref, which, q):
+        return lambda h: ref.at[which, h, :, cuts[q]]
 
     def cov_step(step, carry):
         slot = step % 2
@@ -204,24 +206,39 @@
     loads[1].wait()
     project(gw, gate, False)
     pl.semaphore_wait(barrier, len(peers))
-    g_far = ring_far(gate_data, buf(ra1, 0), x, dev_x)
+    g_far = [ring_far(gate_data(q), buf(ra1, 0, q), x, dev_x) for q in (0, 1)]
     loads[2].wait()
     project(uw, up, True)
-    u_far = ring_far(up_data, buf(ra1, 1), y, dev_y)
-    lax.fori_loop(0, 6, cov_step, 0)
-    g_near = ring_near(gate_data, buf(rb1, 0), x, dev_x)
-    lax.fori_loop(6, 7, cov_step, 0)
-    u_near = ring_near(up_data, buf(rb1, 1), y, dev_y)
-    lax.fori_loop(7, 10, cov_step, 0)
-    g_near += ring_middle(g_far, gate_data, buf(ra1, 0), buf(rc1, 0), x, dev_x)
-    u_near += ring_middle(u_far, up_data, buf(ra1, 1), buf(rc1, 1), y, dev_y)
-    lax.fori_loop(10, COV_STEPS, cov_step, 0)
-    ring_end(g_near, gate_data, buf(rb1, 0), buf(rc1, 0), x)
-    g2 = to_three(lambda d: gate.at[:, x, (y + d) % 4], lambda d: ra2.at[0, d - 1], dev_y)
-    ring_end(u_near, up_data, buf(rb1, 1), buf(rc1, 1), y)
-    u2 = to_three(lambda d: up.at[:, y, (x + d) % 4], lambda d: ra2.at[1, d - 1], dev_x)
-    wait_all(g2)
-    wait_all(u2)
+    u_far = [ring_far(up_data(q), buf(ra1, 1, q), y, dev_y) for q in (0, 1)]
+
+    def near(q):
+        g = ring_near(gate_data(q), buf(rb1, 0, q), x, dev_x)
+        return g, ring_near(up_data(q), buf(rb1, 1, q), y, dev_y)
+
+    def middle(q):
+        g = ring_middle(g_far[q], gate_data(q), buf(ra1, 0, q), buf(rc1, 0, q), x, dev_x)
+        return g, ring_middle(u_far[q], up_data(q), buf(ra1, 1, q), buf(rc1, 1, q), y, dev_y)
+
+    def second(q, g, u):
+        ring_end(g, gate_data(q), buf(rb1, 0, q), buf(rc1, 0, q), x)
+        g2 = to_three(
+            lambda d: gate.at[:, x, (y + d) % 4, cuts[q]], lambda d: ra2.at[0, d - 1, :, cuts[q]], dev_y
+        )
+        ring_end(u, up_data(q), buf(rb1, 1, q), buf(rc1, 1, q), y)
+        return g2 + to_three(
+            lambda d: up.at[:, y, (x + d) % 4, cuts[q]], lambda d: ra2.at[1, d - 1, :, cuts[q]], dev_x
+        )
+
+    lax.fori_loop(0, 5, cov_step, 0)
+    gn0, un0 = near(0)
+    lax.fori_loop(5, 8, cov_step, 0)
+    gc0, uc0 = middle(0)
+    gn1, un1 = near(1)
+    gc1, uc1 = middle(1)
+    lax.fori_loop(8, COV_STEPS, cov_step, 0)
+    parts = second(0, gn0 + gc0, un0 + uc0)
+    parts += second(1, gn1 + gc1, un1 + uc1)
+    wait_all(parts)
 
     keys = jnp.zeros((PIECE, E), F32)
     for p in (0, 1):

time: 125 us -> 124 us (level)
  Pallas kernels: 122 us -> 120 us
    pallas_call x1, Pallas kernels: 122 us -> 120 us  [body(): pl.pallas_call(kernel, out_shape=jax.ShapeDtypeStruct((PIECE, D), BF16),...]
where the time goes in v7:
time: 124 us; the launch traced here: 123 us
  Pallas kernels  120 us (97%)
  local copies, waits for them, and re-layouts  2.83 us (2%)
    pallas_call x1, Pallas kernels, body(): pl.pallas_call(kernel, out_shape=jax.ShapeDtypeStruct((PIECE, D), BF16),...  120 us
    unnamed x1, local copies, waits for them, and re-layouts  2.83 us

profile of v7, /device:TPU:1, one launch (start us, length us, event | category | flops | bytes accessed | tf_op | source)
XLA Modules:
  0.0 123.2 jit_solution(8533840128382994995)
XLA Ops:
  0.0 120.3 %edit.1 = bf16[168,5376]{1,0:T(8,128)(2,1)} custom-call(bf16[2,8,336,128]{3,2,1,0:T(8,128)(2,1)} %bitcast.12, s32[2,128]{1,0:T(2,128)} %bitcast.13, bf16[336,2688]{1,0:T(8,128)(2,1)} %bitcast.9, bf16[336,2688]{1,0:T(8,128)(2,1)} %bitcast.10, bf16[168,5376]{1,0:T(8,128)(2,1)} %bitcast.11, f32[28224,128]{1,0:T(8,128)} %bitcast.7, f32[42,128]{1,0:T(8,128)} %tgt.1), custom_call_target="tpu_custom_call" | custom-call | tf_op jit(solution)/shard_map/edit/pallas_call | solution.py:507
  120.3 2.8 %copy.9 = bf16[1,1,168,5376]{3,2,1,0:T(8,128)(2,1)} copy(bf16[1,1,168,5376]{3,2,1,0:T(8,128)(2,1)} %bitcast.8) | data formatting | bytes 3612672

commit v8 on v7

--- a/solution.py
+++ b/solution.py
@@ -283,7 +283,7 @@
             rows = pl.ds(pl.multiple_of(i * 336, 16), 336)
             return total + dot_tb(left[rows, :], right[rows, :])
 
-        total = lax.fori_loop(0, 8, body, jnp.zeros((2 * E, 2 * E), F32))
+        total = lax.fori_loop(0, 8, body, jnp.zeros((2 * E, 2 * E), F32), unroll=2)
         return (total[:E, :E] + total[E:, E:]) + (total[:E, E:] + total[E:, :E])
 
     def cov_times(i, target):
@@ -378,7 +378,7 @@
         vv[i, 1] = value[PIECE:]
         return carry
 
-    lax.fori_loop(0, 4, first_image, 0)
+    lax.fori_loop(0, 4, first_image, 0, unroll=2)
     v1 = cp(vv.at[:, 1 - k], vk, dev_k)
     v1.wait_recv()
     vv[:, k] += vk[...]
@@ -433,10 +433,10 @@
         value = cov_times(i, whl)
         return total + dot_t(wr[i].reshape(336, E), value)
 
-    total = lax.fori_loop(0, 2, second_image, jnp.zeros((E, E), F32))
+    total = lax.fori_loop(0, 2, second_image, jnp.zeros((E, E), F32), unroll=2)
     cores_end(nk, first_n, 1, nc.at[pl.ds(0, 1)])
     nz = axis_start(first_n, 1, nzr.at[0], dev_z)
-    total = lax.fori_loop(2, 4, second_image, total)
+    total = lax.fori_loop(2, 4, second_image, total, unroll=2)
     halve(n3, 0, total)
     n3k = cores_start(n3, 1, mc2)
     cores_end(n3k, n3, 1, mc2)

time: 124 us -> 122 us (0.984)
  no operation moved by 1% of the time
where the time goes in v8:
time: 122 us
  Pallas kernels  119 us (98%)
  local copies, waits for them, and re-layouts  2.83 us (2%)
    pallas_call x1, Pallas kernels, body(): pl.pallas_call(kernel, out_shape=jax.ShapeDtypeStruct((PIECE, D), BF16),...  119 us
    unnamed x1, local copies, waits for them, and re-layouts  2.83 us

profile of v8, /device:TPU:1, one launch (start us, length us, event | category | flops | bytes accessed | tf_op | source)
XLA Modules:
  0.0 121.9 jit_solution(13989200139418599643)
XLA Ops:
  0.0 119.1 %edit.1 = bf16[168,5376]{1,0:T(8,128)(2,1)} custom-call(bf16[2,8,336,128]{3,2,1,0:T(8,128)(2,1)} %bitcast.12, s32[2,128]{1,0:T(2,128)} %bitcast.13, bf16[336,2688]{1,0:T(8,128)(2,1)} %bitcast.9, bf16[336,2688]{1,0:T(8,128)(2,1)} %bitcast.10, bf16[168,5376]{1,0:T(8,128)(2,1)} %bitcast.11, f32[28224,128]{1,0:T(8,128)} %bitcast.7, f32[42,128]{1,0:T(8,128)} %tgt.1), custom_call_target="tpu_custom_call" | custom-call | tf_op jit(solution)/shard_map/edit/pallas_call | solution.py:507
  119.1 2.8 %copy.9 = bf16[1,1,168,5376]{3,2,1,0:T(8,128)(2,1)} copy(bf16[1,1,168,5376]{3,2,1,0:T(8,128)(2,1)} %bitcast.8) | data formatting | bytes 3612672
